TPU v7x, 512 devices: a whole 4x4x16 slice. The times are simulated.
512 devices in a mesh: depth: 8 (over x, core), lat: 64 (over z, y).
Axes of the slice: x: 4, y: 4, z: 16, core: 2. Of those that a mesh axis runs over, the one named last changes fastest.
Arguments:
- object_field: bfloat16 [2, 64, 8192, 256], P(None, 'depth', 'lat'), may hold values from -6 to 6
- probe_field: bfloat16 [2, 128, 256], replicated, may hold values from -6 to 6
- intensity: bfloat16 [512, 128, 256], P('lat'), may hold values from 0.099609375 to 4
- depth_phase: float32 [32, 64], P(None, 'depth'), may hold values from -3.140625 to 3.140625
- shear_rate: int32 [32], replicated, may hold values from -64 to 64
- positions: int32 [512], P('lat'), may hold values from -32 to 32
- angle_index: int32 [512], P('lat'), may hold values from 0 to 31
- frame_count: int32 [64], P('lat'), may hold values from 1 to 8, 320 in all
Outputs:
- correction: float32 [2, 64, 8192, 256], P(None, 'depth', 'lat')
Inputs may be any that keep to these rules, and one draw needn't show every extreme that they name: `frame_count`: some tile owns all 8 slots' frames in every draw.
All inputs are finite; a program needn't handle non-finite values. No bound on the sum of `frame_count` on one device may be relied on, other than what follows from the above.
Results may differ from a plain program's by a relative error of at most 0.0003.
Values may be sent and summed in bfloat16 or wider, within the bound.
No kernel may reach another device: no remote copies, remote signals or barrier semaphores. Data moves between devices by JAX's collectives and lax.ppermute only.
A program may use at most 64 MiB of HBM per device.

v0:
```python
import math

import jax
import jax.numpy as jnp
import ml_dtypes
import numpy as np
from jax import lax
from jax.experimental import pallas as pl
from jax.experimental.pallas import tpu as pltpu
from jax.sharding import PartitionSpec as P

INTERPRET = False
LANES = 128
HEAD = 16
STEPS = 128.0
TOP = 32700.0
SHIFTER = 12582912.0


def split_pair(table):
    high = table.astype(ml_dtypes.bfloat16)
    low = (table - high.astype(np.float64)).astype(ml_dtypes.bfloat16)
    return high, low


def dft_pair(length):
    index = np.arange(length, dtype=np.int64)
    theta = 2.0 * np.pi / length * (index[:, None] * index[None, :] % length)
    factor = 1.0 / math.sqrt(length)
    return np.cos(theta) * factor, np.sin(theta) * factor


def row_table(length):
    high, low = split_pair(np.concatenate(dft_pair(length), axis=0))
    return np.concatenate([high, low, high], axis=1)


def column_tables(length):
    return split_pair(np.concatenate(dft_pair(length), axis=1))


def column_code(peak):
    bounded = jnp.maximum(peak, 2.0**-100)
    return jnp.ceil(jnp.log(bounded) * (STEPS / math.log(2.0))) + 1.0


def code_gain(code):
    return TOP * jnp.exp(code * (-math.log(2.0) / STEPS))


def code_step(code):
    return jnp.exp(code * (math.log(2.0) / STEPS)) * (1.0 / TOP)


def coded(value, gain):
    rounded = (value * gain + SHIFTER) - SHIFTER
    return rounded.astype(jnp.int32).astype(jnp.int16)


def widened(value):
    return value.astype(jnp.int32).astype(jnp.float32)


def shift_of(shear, level, total):
    return lax.shift_right_arithmetic(shear * (2 * level - total), int(math.log2(2 * total)))


def exit_kernel(
    slab, positions, angles, shears, cosines, sines, own, low, high, out, extended, wave, *, total
):
    frame = pl.program_id(0)
    levels, tile = own.shape[1], own.shape[2]
    reach = tile // 2
    halves = own.shape[3] // LANES

    @pl.when(frame == 0)
    def _():
        def fill(level, carry):
            for part in range(2):
                rim = pl.ds((part * levels + level) * reach, reach)
                for half in range(halves):
                    lanes = slice(half * LANES, (half + 1) * LANES)
                    extended[part, level, half, :reach] = low[rim, lanes].astype(jnp.float32)
                    extended[part, level, half, reach : reach + tile] = own[
                        part, level, :, lanes
                    ].astype(jnp.float32)
                    extended[part, level, half, reach + tile :] = high[rim, lanes].astype(
                        jnp.float32
                    )
            return carry

        lax.fori_loop(0, levels, fill, 0)

    angle = angles[frame]
    shear = shears[angle]
    base = reach + positions[frame]
    first = slab[0] * levels
    starts = [base + shift_of(shear, first + level, total) for level in range(levels)]
    ramps = [(cosines[angle, level], sines[angle, level]) for level in range(levels)]
    for half in range(halves):
        lanes = slice(half * LANES, (half + 1) * LANES)
        peak = jnp.zeros((1, LANES), jnp.float32)
        for chunk in range(2):
            sum_real = jnp.zeros((reach, LANES), jnp.float32)
            sum_imag = jnp.zeros((reach, LANES), jnp.float32)
            for level in range(levels):
                rows = pl.ds(starts[level] + chunk * reach, reach)
                real = extended[0, level, half, rows]
                imag = extended[1, level, half, rows]
                ramp_real, ramp_imag = ramps[level]
                sum_real = sum_real + (real * ramp_real - imag * ramp_imag)
                sum_imag = sum_imag + (real * ramp_imag + imag * ramp_real)
            wave[0, chunk] = sum_real
            wave[1, chunk] = sum_imag
            top = jnp.maximum(jnp.abs(sum_real), jnp.abs(sum_imag))
            peak = jnp.maximum(peak, jnp.max(top, axis=0, keepdims=True))
        code = column_code(peak)
        gain = code_gain(code)
        for part in range(2):
            for chunk in range(2):
                at = (part * 2 + chunk) * reach
                out[0, at : at + reach, lanes] = coded(wave[part, chunk], gain)
        out[0, 4 * reach :, lanes] = (
            jnp.broadcast_to(code, (HEAD, LANES)).astype(jnp.int32).astype(jnp.int16)
        )


def halves_of(value):
    high = value.astype(jnp.bfloat16)
    low = (value - high.astype(jnp.float32)).astype(jnp.bfloat16)
    return high, low


def matmul(left, right):
    return jnp.dot(left, right, preferred_element_type=jnp.float32)


def row_products(table, real, imag):
    high, low = halves_of(jnp.concatenate([real, imag], axis=1))
    both = matmul(table[...], jnp.concatenate([high, high, low], axis=0))
    rows, columns = real.shape
    return (
        both[:rows, :columns],
        both[:rows, columns:],
        both[rows:, :columns],
        both[rows:, columns:],
    )


def column_products(table_high, table_low, real, imag):
    high, low = halves_of(jnp.concatenate([real, imag], axis=0))
    both = matmul(high, table_high[...])
    both = both + matmul(high, table_low[...])
    both = both + matmul(low, table_high[...])
    rows, columns = real.shape
    return (
        both[:rows, :columns],
        both[rows:, :columns],
        both[:rows, columns:],
        both[rows:, columns:],
    )


def frame_kernel(
    slot, count, partials, probe, intensity, row_ref, column_high, column_low, out, *, total
):
    frames = partials.shape[0]
    tile = probe.shape[1]
    reach = tile // 2
    sum_real = jnp.zeros(probe.shape[1:], jnp.float32)
    sum_imag = jnp.zeros(probe.shape[1:], jnp.float32)
    for source in range(frames):
        step = code_step(widened(partials[source, 4 * reach :])[:1])
        sum_real = sum_real + widened(partials[source, : 2 * reach]) * step
        sum_imag = sum_imag + widened(partials[source, 2 * reach : 4 * reach]) * step
    scale = 1.0 / math.sqrt(total)
    sum_real = sum_real * scale
    sum_imag = sum_imag * scale
    probe_real = probe[0].astype(jnp.float32)
    probe_imag = probe[1].astype(jnp.float32)
    wave_real = probe_real * sum_real - probe_imag * sum_imag
    wave_imag = probe_real * sum_imag + probe_imag * sum_real

    cos_real, cos_imag, sin_real, sin_imag = row_products(row_ref, wave_real, wave_imag)
    mid_real = cos_real + sin_imag
    mid_imag = cos_imag - sin_real
    cos_real, cos_imag, sin_real, sin_imag = column_products(
        column_high, column_low, mid_real, mid_imag
    )
    far_real = cos_real + sin_imag
    far_imag = cos_imag - sin_real

    magnitude = jnp.sqrt(far_real * far_real + far_imag * far_imag)
    amplitude = jnp.sqrt(intensity[0].astype(jnp.float32))
    valid = jnp.where(slot[0] < count[0], 1.0, 0.0).astype(jnp.float32)
    factor = (amplitude / jnp.maximum(magnitude, 0.5) - 1.0) * valid
    far_real = far_real * factor
    far_imag = far_imag * factor

    cos_real, cos_imag, sin_real, sin_imag = column_products(
        column_high, column_low, far_real, far_imag
    )
    mid_real = cos_real - sin_imag
    mid_imag = cos_imag + sin_real
    cos_real, cos_imag, sin_real, sin_imag = row_products(row_ref, mid_real, mid_imag)
    update_real = cos_real - sin_imag
    update_imag = cos_imag + sin_real

    back_real = probe_real * update_real + probe_imag * update_imag
    back_imag = probe_real * update_imag - probe_imag * update_real
    peak = jnp.max(
        jnp.maximum(jnp.abs(back_real), jnp.abs(back_imag)), axis=0, keepdims=True
    )
    code = column_code(peak)
    gain = code_gain(code)
    coded_real = coded(back_real, gain)
    coded_imag = coded(back_imag, gain)
    out[:reach] = coded_real[:reach]
    out[reach : 2 * reach] = coded_imag[:reach]
    out[2 * reach : 2 * reach + HEAD] = (
        jnp.broadcast_to(code, (HEAD, code.shape[1])).astype(jnp.int32).astype(jnp.int16)
    )
    out[2 * reach + HEAD : 3 * reach + HEAD] = coded_real[reach:]
    out[3 * reach + HEAD :] = coded_imag[reach:]


def own_kernel(
    slab, positions, angles, shears, cosines, sines, frames_ref, out, padded, *, total
):
    level = pl.program_id(0)
    levels = pl.num_programs(0)
    frames, tile = frames_ref.shape[0], out.shape[2]
    reach = tile // 2
    halves = out.shape[3] // LANES

    @pl.when(level == 0)
    def _():
        blank = jnp.zeros((reach, LANES), jnp.float32)

        def fill(frame, carry):
            for half in range(halves):
                lanes = slice(half * LANES, (half + 1) * LANES)
                head = frames_ref[frame, 2 * reach : 2 * reach + HEAD, lanes]
                step = code_step(widened(head)[:1])
                for part in range(2):
                    padded[part, frame, half, :reach] = blank
                    padded[part, frame, half, reach + tile :] = blank
                    at = part * reach
                    padded[part, frame, half, reach : 2 * reach] = (
                        widened(frames_ref[frame, at : at + reach, lanes]) * step
                    )
                    at = (2 + part) * reach + HEAD
                    padded[part, frame, half, 2 * reach : 3 * reach] = (
                        widened(frames_ref[frame, at : at + reach, lanes]) * step
                    )
            return carry

        lax.fori_loop(0, frames, fill, 0)

    here = slab[0] * levels + level
    starts, ramps = [], []
    for frame in range(frames):
        angle = angles[frame]
        starts.append(reach - positions[frame] - shift_of(shears[angle], here, total))
        ramps.append((cosines[angle, level], sines[angle, level]))
    for half in range(halves):
        lanes = slice(half * LANES, (half + 1) * LANES)
        for chunk in range(2):
            sum_real = jnp.zeros((reach, LANES), jnp.float32)
            sum_imag = jnp.zeros((reach, LANES), jnp.float32)
            for frame in range(frames):
                rows = pl.ds(starts[frame] + chunk * reach, reach)
                real = padded[0, frame, half, rows]
                imag = padded[1, frame, half, rows]
                ramp_real, ramp_imag = ramps[frame]
                sum_real = sum_real + (real * ramp_real + imag * ramp_imag)
                sum_imag = sum_imag + (imag * ramp_real - real * ramp_imag)
            rows = slice(chunk * reach, (chunk + 1) * reach)
            out[0, 0, rows, lanes] = sum_real
            out[1, 0, rows, lanes] = sum_imag


def rim_kernel(
    slab, below, above, shears, cosines, sines, lower, upper, inner, out, padded, *, total
):
    level = pl.program_id(0)
    levels = pl.num_programs(0)
    frames, tile = lower.shape[0], out.shape[2]
    reach = tile // 2
    halves = out.shape[3] // LANES

    @pl.when(level == 0)
    def _():
        blank = jnp.zeros((reach, LANES), jnp.float32)

        def fill(frame, carry):
            for half in range(halves):
                lanes = slice(half * LANES, (half + 1) * LANES)
                low_step = code_step(widened(lower[frame, :HEAD, lanes])[:1])
                high_step = code_step(widened(upper[frame, 2 * reach :, lanes])[:1])
                for part in range(2):
                    at = HEAD + part * reach
                    padded[0, part, frame, half, :reach] = (
                        widened(lower[frame, at : at + reach, lanes]) * low_step
                    )
                    padded[0, part, frame, half, reach:] = blank
                    at = part * reach
                    padded[1, part, frame, half, :reach] = blank
                    padded[1, part, frame, half, reach:] = (
                        widened(upper[frame, at : at + reach, lanes]) * high_step
                    )
            return carry

        lax.fori_loop(0, frames, fill, 0)

    here = slab[0] * levels + level
    for chunk, around in enumerate((below, above)):
        starts, ramps = [], []
        for frame in range(frames):
            angle = around[frames + frame]
            start = around[frame] + shift_of(shears[angle], here, total)
            if chunk == 0:
                starts.append(reach - jnp.maximum(start, 0))
            else:
                starts.append(-jnp.minimum(start, 0))
            ramps.append((cosines[angle, level], sines[angle, level]))
        for half in range(halves):
            lanes = slice(half * LANES, (half + 1) * LANES)
            at = slice(chunk * reach, (chunk + 1) * reach)
            sum_real = inner[0, 0, at, lanes]
            sum_imag = inner[1, 0, at, lanes]
            for frame in range(frames):
                rows = pl.ds(starts[frame], reach)
                real = padded[chunk, 0, frame, half, rows]
                imag = padded[chunk, 1, frame, half, rows]
                ramp_real, ramp_imag = ramps[frame]
                sum_real = sum_real + (real * ramp_real + imag * ramp_imag)
                sum_imag = sum_imag + (imag * ramp_real - real * ramp_imag)
            out[0, 0, at, lanes] = sum_real
            out[1, 0, at, lanes] = sum_imag


def scalars():
    return pl.BlockSpec(memory_space=pltpu.SMEM)


def resident(shape):
    return pl.BlockSpec(shape, lambda *_: (0,) * len(shape), pipeline_mode=pl.Buffered(1))


def params(mebibytes):
    return pltpu.CompilerParams(vmem_limit_bytes=mebibytes << 20)


def passed_along(value, steps):
    count = lax.axis_size("lat")
    initial, last = (max(0, -steps), min(count, count - steps))
    return lax.ppermute(value, "lat", [(source, source + steps) for source in range(initial, last)])


def shards(
    object_field,
    probe_field,
    intensity,
    depth_phase,
    shear_rate,
    positions,
    angle_index,
    frame_count,
):
    levels = object_field.shape[1]
    tile = object_field.shape[2]
    width = object_field.shape[3]
    frames = positions.shape[0]
    reach = tile // 2
    halves = width // LANES
    slabs = lax.axis_size("depth")
    total = levels * slabs
    slab = lax.axis_index("depth").astype(jnp.int32).reshape(1)
    coded_rows = 2 * tile + HEAD

    spots = jnp.concatenate([positions, angle_index]).astype(jnp.bfloat16)
    spots = jnp.pad(spots[None], ((0, HEAD - 1), (0, width - 2 * frames)))
    rim_rows = 2 * levels * reach
    last = jnp.concatenate([object_field[:, :, reach:].reshape(rim_rows, width), spots])
    start = jnp.concatenate([object_field[:, :, :reach].reshape(rim_rows, width), spots])
    low = passed_along(last, 1)
    high = passed_along(start, -1)
    below = low[rim_rows, : 2 * frames].astype(jnp.int32)
    above = high[rim_rows, : 2 * frames].astype(jnp.int32)
    cosines = jnp.cos(depth_phase)
    sines = jnp.sin(depth_phase)

    partials = pl.pallas_call(
        lambda *refs: exit_kernel(*refs, total=total),
        out_shape=jax.ShapeDtypeStruct((frames, coded_rows, width), jnp.int16),
        grid=(frames,),
        in_specs=[scalars()] * 6
        + [
            resident(object_field.shape),
            resident(low.shape),
            resident(high.shape),
        ],
        out_specs=pl.BlockSpec((1, coded_rows, width), lambda f: (f, 0, 0)),
        scratch_shapes=[
            pltpu.VMEM((2, levels, halves, 2 * tile, LANES), jnp.float32),
            pltpu.VMEM((2, 2, reach, LANES), jnp.float32),
        ],
        compiler_params=params(16),
        interpret=INTERPRET,
        name="exit_waves",
    )(slab, positions, angle_index, shear_rate, cosines, sines, object_field, low, high)

    received = lax.all_to_all(partials, "depth", 0, 0)

    table = jnp.asarray(row_table(tile))
    column_high, column_low = (jnp.asarray(t) for t in column_tables(width))
    back = pl.pallas_call(
        lambda *refs: frame_kernel(*refs, total=total),
        out_shape=jax.ShapeDtypeStruct((coded_rows, width), jnp.int16),
        grid_spec=pltpu.PrefetchScalarGridSpec(
            num_scalar_prefetch=2,
            grid=(1,),
            in_specs=[
                resident(received.shape),
                resident(probe_field.shape),
                pl.BlockSpec((1, tile, width), lambda i, slot, count: (slot[0], 0, 0)),
                resident(table.shape),
                resident(column_high.shape),
                resident(column_low.shape),
            ],
            out_specs=pl.BlockSpec((coded_rows, width), lambda *_: (0, 0)),
        ),
        compiler_params=params(16),
        interpret=INTERPRET,
        name="far_field",
    )(slab, frame_count, received, probe_field, intensity, table, column_high, column_low)

    gathered = lax.all_gather(back, "depth")
    lower = passed_along(gathered[:, tile:], 1)
    upper = passed_along(gathered[:, : tile + HEAD], -1)

    level_block = pl.BlockSpec((2, 1, tile, width), lambda z: (0, z, 0, 0))
    shape = jax.ShapeDtypeStruct((2, levels, tile, width), jnp.float32)
    inner = pl.pallas_call(
        lambda *refs: own_kernel(*refs, total=total),
        out_shape=shape,
        grid=(levels,),
        in_specs=[scalars()] * 6 + [resident(gathered.shape)],
        out_specs=level_block,
        scratch_shapes=[pltpu.VMEM((2, frames, halves, 2 * tile, LANES), jnp.float32)],
        compiler_params=params(16),
        cost_estimate=pl.CostEstimate(
            flops=frames * levels * tile * width * 8, bytes_accessed=4 << 20, transcendentals=0
        ),
        interpret=INTERPRET,
        name="own_frames",
    )(slab, positions, angle_index, shear_rate, cosines, sines, gathered)

    return pl.pallas_call(
        lambda *refs: rim_kernel(*refs, total=total),
        out_shape=shape,
        grid=(levels,),
        in_specs=[scalars()] * 6
        + [
            resident(lower.shape),
            resident(upper.shape),
            level_block,
        ],
        out_specs=level_block,
        scratch_shapes=[pltpu.VMEM((2, 2, frames, halves, tile, LANES), jnp.float32)],
        compiler_params=params(16),
        interpret=INTERPRET,
        name="neighbour_frames",
    )(slab, below, above, shear_rate, cosines, sines, lower, upper, inner)


def solution(mesh):
    placed = (
        P(None, "depth", "lat", None),
        P(),
        P("lat", None, None),
        P(None, "depth"),
        P(),
        P("lat"),
        P("lat"),
        P("lat"),
    )
    return jax.shard_map(
        shards, mesh=mesh, in_specs=placed, out_specs=P(None, "depth", "lat", None), check_vma=False
    )
```

profile of v0, /device:TPU:385, one launch (start us, length us, event | category | flops | bytes accessed | tf_op | source)
XLA Modules:
  0.0 101.3 jit_solution(367005695347033039)
XLA Ops:
  0.0 1.3 %fusion.9 = (bf16[2,8,64,256]{3,2,1,0:T(8,128)(2,1)S(1)}, bf16[2,8,64,256]{3,2,1,0:T(8,128)(2,1)S(1)}) fusion(bf16[2,8,128,256]{3,2,1,0:T(8,128)(2,1)} %refs_6_.2), kind=kLoop, calls=%fused_computation.17 | loop fusion | bytes 2097152 | tf_op jit(solution)/shard_map/slice | solution.py:386
  1.3 0.0 copy-done.7
  1.3 0.0 copy-done.8
  1.3 0.0 copy-start.9
  1.4 0.0 copy-start
  1.4 0.0 copy-start.6
  1.4 0.1 fusion.5
  1.5 0.9 pad_maximum_fusion
  2.3 6.3 %collective-permute-start.1 = (bf16[1040,256]{1,0:T(8,128)(2,1)}, bf16[1040,256]{1,0:T(8,128)(2,1)S(1)}, u32[]{:S(2)}, u32[]{:S(2)}) collective-permute-start(bf16[1040,256]{1,0:T(8,128)(2,1)} %get-tuple-element.11), channel_id=1, source_target_pairs={{1,0},{2,1},{3,2},{4,3},{5,4},{6,5},{7,6},{8,7},{9,8},{10,9},{11,1... | collective-permute-start | bytes 1597448 | tf_op jit(solution)/shard_map/ppermute | solution.py:358
  8.6 1.9 %collective-permute-start = (bf16[1040,256]{1,0:T(8,128)(2,1)S(1)}, bf16[1040,256]{1,0:T(8,128)(2,1)S(1)}, u32[]{:S(2)}, u32[]{:S(2)}) collective-permute-start(bf16[1040,256]{1,0:T(8,128)(2,1)S(1)} %get-tuple-element.12), channel_id=1, source_target_pairs={{0,1},{1,2},{2,3},{3,4},{4,5},{5,6},{6,7},{7,8},{8,9},{9,10},{10,1... | collective-permute-start | bytes 1597448 | tf_op jit(solution)/shard_map/ppermute | solution.py:358
  10.6 0.1 copy.12
  10.6 0.1 fusion.10
  10.7 9.0 %collective-permute-done.1.refs_8_ = bf16[1040,256]{1,0:T(8,128)(2,1)S(1)} collective-permute-done((bf16[1040,256]{1,0:T(8,128)(2,1)}, bf16[1040,256]{1,0:T(8,128)(2,1)S(1)}, u32[]{:S(2)}, u32[]{:S(2)}) %collective-permute-start.1) | collective-permute-done | bytes 532512 | tf_op jit(solution)/shard_map/ppermute | solution.py:358
  19.7 6.8 %collective-permute-done.refs_7_ = bf16[1040,256]{1,0:T(8,128)(2,1)S(1)} collective-permute-done((bf16[1040,256]{1,0:T(8,128)(2,1)S(1)}, bf16[1040,256]{1,0:T(8,128)(2,1)S(1)}, u32[]{:S(2)}, u32[]{:S(2)}) %collective-permute-start) | collective-permute-done | bytes 532512 | tf_op jit(solution)/shard_map/ppermute | solution.py:358
  26.5 0.0 copy-done.6
  26.5 6.0 %exit_waves.1 = s16[8,272,256]{2,1,0:T(8,128)(2,1)} custom-call(s32[1]{0:T(128)} %bitcast.refs_0_, s32[8]{0:T(128)S(1)} %copy-done.8, s32[8]{0:T(128)S(1)} %copy-done.7, s32[32]{0:T(128)S(1)} %copy-done.6, f32[32,8]{1,0:T(8,128)S(1)} %get-tuple-element.10.refs_4_, f32[32,8]{1,0:T(8,128)S(1)} %get-tuple-element.9.refs_5_, ...), custom_call_target="tpu_custom_call" | custom-call | tf_op jit(solution)/shard_map/exit_waves/pallas_call | solution.py:394
  32.5 0.0 copy-start.4
  32.5 6.3 %all-to-all-start = ((s16[8,272,256]{2,1,0:T(8,128)(2,1)}), s16[8,272,256]{2,1,0:T(8,128)(2,1)S(1)}, u32[]{:S(2)}, u32[]{:S(2)}) async-start(s16[8,272,256]{2,1,0:T(8,128)(2,1)} %exit_waves.1), calls=%async_computation | async-start | bytes 2228224 | tf_op jit(solution)/shard_map/all_to_all | solution.py:414
  39.5 15.2 %all-to-all-done.refs_2_ = s16[8,272,256]{2,1,0:T(8,128)(2,1)S(1)} async-done(((s16[8,272,256]{2,1,0:T(8,128)(2,1)}), s16[8,272,256]{2,1,0:T(8,128)(2,1)S(1)}, u32[]{:S(2)}, u32[]{:S(2)}) %all-to-all-start) | async-done | bytes 1114144 | tf_op jit(solution)/shard_map/all_to_all | solution.py:414
  54.7 0.0 copy-done.1
  54.7 0.0 copy-done.3
  54.7 0.0 copy-start.5
  54.7 0.9 copy-done.5
  55.6 2.2 %far_field.1 = s16[272,256]{1,0:T(8,128)(2,1)S(1)} custom-call(s32[1]{0:T(128)} %bitcast.refs_0_, s32[1]{0:T(128)S(6)} %copy.14.refs_1_, s16[8,272,256]{2,1,0:T(8,128)(2,1)S(1)} %all-to-all-done.refs_2_, bf16[2,128,256]{2,1,0:T(8,128)(2,1)S(1)} %copy-done.5, bf16[8,128,256]{2,1,0:T(8,128)(2,1)S(1)} %copy-done.1, bf16[256,384]{1,0:T(8,128)(2,1)S(1)} %copy-done.4, ...), custom_call_target="tpu_custom_call" | custom-call | tf_op jit(solution)/shard_map/far_field/pallas_call | solution.py:418
  57.8 14.7 %all-gather.2 = s16[2176,256]{1,0:T(8,128)(2,1)S(1)} all-gather(s16[272,256]{1,0:T(8,128)(2,1)S(1)} %far_field.1), channel_id=2, replica_groups=mesh['depth'=8,'lat'=64] {'depth'}, dimensions={0}, use_global_device_ids=true | all-gather | bytes 1253376 | tf_op jit(solution)/shard_map/all_gather | solution.py:439
  72.6 0.1 fusion.8
  72.6 1.9 %collective-permute-start.3 = (s16[8,144,256]{2,1,0:T(8,128)(2,1)S(1)}, s16[8,144,256]{2,1,0:T(8,128)(2,1)S(1)}, u32[]{:S(2)}, u32[]{:S(2)}) collective-permute-start(s16[8,144,256]{2,1,0:T(8,128)(2,1)S(1)} %get-tuple-element.5), channel_id=1, source_target_pairs={{1,0},{2,1},{3,2},{4,3},{5,4},{6,5},{7,6},{8,7},{9,8},{10,9},{11,1... | collective-permute-start | bytes 1769480 | tf_op jit(solution)/shard_map/ppermute | solution.py:358
  74.6 3.4 %collective-permute-start.2 = (s16[8,144,256]{2,1,0:T(8,128)(2,1)S(1)}, s16[8,144,256]{2,1,0:T(8,128)(2,1)S(1)}, u32[]{:S(2)}, u32[]{:S(2)}) collective-permute-start(s16[8,144,256]{2,1,0:T(8,128)(2,1)S(1)} %get-tuple-element.6), channel_id=1, source_target_pairs={{0,1},{1,2},{2,3},{3,4},{4,5},{5,6},{6,7},{7,8},{8,9},{9,10},{10,1... | collective-permute-start | bytes 1769480 | tf_op jit(solution)/shard_map/ppermute | solution.py:358
  78.0 5.5 %own_frames.1.refs_8_ = f32[2,8,128,256]{3,2,1,0:T(8,128)S(1)} custom-call(s32[1]{0:T(128)} %bitcast.refs_0_, s32[8]{0:T(128)S(1)} %copy-done.8, s32[8]{0:T(128)S(1)} %copy-done.7, s32[32]{0:T(128)S(1)} %copy-done.6, f32[32,8]{1,0:T(8,128)S(1)} %get-tuple-element.10.refs_4_, f32[32,8]{1,0:T(8,128)S(1)} %get-tuple-element.9.refs_5_, ...), custom_call_target="tpu_custom_call" | custom-call | flops 16777216 | bytes 4194304 | tf_op jit(solution)/shard_map/own_frames/pallas_call | solution.py:445
  83.5 5.9 %collective-permute-done.3.refs_7_ = s16[8,144,256]{2,1,0:T(8,128)(2,1)S(1)} collective-permute-done((s16[8,144,256]{2,1,0:T(8,128)(2,1)S(1)}, s16[8,144,256]{2,1,0:T(8,128)(2,1)S(1)}, u32[]{:S(2)}, u32[]{:S(2)}) %collective-permute-start.3) | collective-permute-done | bytes 589856 | tf_op jit(solution)/shard_map/ppermute | solution.py:358
  89.3 5.2 %collective-permute-done.2.refs_6_ = s16[8,144,256]{2,1,0:T(8,128)(2,1)S(1)} collective-permute-done((s16[8,144,256]{2,1,0:T(8,128)(2,1)S(1)}, s16[8,144,256]{2,1,0:T(8,128)(2,1)S(1)}, u32[]{:S(2)}, u32[]{:S(2)}) %collective-permute-start.2) | collective-permute-done | bytes 589856 | tf_op jit(solution)/shard_map/ppermute | solution.py:358
  94.6 6.7 %neighbour_frames.1 = f32[2,8,128,256]{3,2,1,0:T(8,128)} custom-call(s32[1]{0:T(128)} %bitcast.refs_0_, s32[16]{0:T(128)S(1)} %fusion.7.refs_1_, s32[16]{0:T(128)S(1)} %fusion.6.refs_2_, s32[32]{0:T(128)S(1)} %copy-done.6, f32[32,8]{1,0:T(8,128)S(1)} %get-tuple-element.10.refs_4_, f32[32,8]{1,0:T(8,128)S(1)} %get-tuple-element.9.refs_5_, ...), custom_call_target="tpu_custom_call" | custom-call | tf_op jit(solution)/shard_map/neighbour_frames/pallas_call | solution.py:460
  (12 shorter events, 0.0 us)
Async XLA Ops:
  0.0 1.3 %copy-start.7 = (s32[8]{0:T(128)S(1)}, s32[8]{0:T(128)}, u32[]{:S(2)}) copy-start(s32[8]{0:T(128)} %refs_2_.3) | copy-start | bytes 100
  0.0 1.3 %copy-start.8 = (s32[8]{0:T(128)S(1)}, s32[8]{0:T(128)}, u32[]{:S(2)}) copy-start(s32[8]{0:T(128)} %refs_1_.4) | copy-start | bytes 100
  1.3 9.2 %copy-start.9 = (f32[32,8]{0,1:T(8,128)S(1)}, f32[32,8]{0,1:T(8,128)}, u32[]{:S(2)}) copy-start(f32[32,8]{0,1:T(8,128)} %param.14) | copy-start | bytes 3076
  1.4 25.1 %copy-start = (bf16[2,8,128,256]{3,2,1,0:T(8,128)(2,1)S(1)}, bf16[2,8,128,256]{3,2,1,0:T(8,128)(2,1)}, u32[]{:S(2)}) copy-start(bf16[2,8,128,256]{3,2,1,0:T(8,128)(2,1)} %refs_6_.2) | copy-start | bytes 3145732
  1.4 25.1 %copy-start.6 = (s32[32]{0:T(128)S(1)}, s32[32]{0:T(128)}, u32[]{:S(2)}) copy-start(s32[32]{0:T(128)} %refs_3_.7) | copy-start | bytes 388
  2.3 17.4 %collective-permute-start.1 = (bf16[1040,256]{1,0:T(8,128)(2,1)}, bf16[1040,256]{1,0:T(8,128)(2,1)S(1)}, u32[]{:S(2)}, u32[]{:S(2)}) collective-permute-start(bf16[1040,256]{1,0:T(8,128)(2,1)} %get-tuple-element.11), channel_id=1, source_target_pairs={{1,0},{2,1},{3,2},{4,3},{5,4},{6,5},{7,6},{8,7},{9,8},{10,9},{11,1... | collective-permute-start | bytes 1597448 | tf_op jit(solution)/shard_map/ppermute | solution.py:358
  8.6 17.9 %collective-permute-start = (bf16[1040,256]{1,0:T(8,128)(2,1)S(1)}, bf16[1040,256]{1,0:T(8,128)(2,1)S(1)}, u32[]{:S(2)}, u32[]{:S(2)}) collective-permute-start(bf16[1040,256]{1,0:T(8,128)(2,1)S(1)} %get-tuple-element.12), channel_id=1, source_target_pairs={{0,1},{1,2},{2,3},{3,4},{4,5},{5,6},{6,7},{7,8},{8,9},{9,10},{10,1... | collective-permute-start | bytes 1597448 | tf_op jit(solution)/shard_map/ppermute | solution.py:358
  32.5 22.1 %copy-start.1 = (bf16[8,128,256]{2,1,0:T(8,128)(2,1)S(1)}, bf16[8,128,256]{2,1,0:T(8,128)(2,1)}, u32[]{:S(2)}) copy-start(bf16[8,128,256]{2,1,0:T(8,128)(2,1)} %refs_4_.1) | copy-start | bytes 1572868
  32.5 22.1 %copy-start.2 = (bf16[256,512]{1,0:T(8,128)(2,1)S(1)}, bf16[256,512]{1,0:T(8,128)(2,1)}, u32[]{:S(2)}) copy-start(bf16[256,512]{1,0:T(8,128)(2,1)} %constant.17.clone.refs_7_) | copy-start | bytes 786436
  32.5 22.1 %copy-start.3 = (bf16[256,512]{1,0:T(8,128)(2,1)S(1)}, bf16[256,512]{1,0:T(8,128)(2,1)}, u32[]{:S(2)}) copy-start(bf16[256,512]{1,0:T(8,128)(2,1)} %constant.16.clone.refs_6_) | copy-start | bytes 786436
  32.5 22.1 %copy-start.4 = (bf16[256,384]{1,0:T(8,128)(2,1)S(1)}, bf16[256,384]{1,0:T(8,128)(2,1)}, u32[]{:S(2)}) copy-start(bf16[256,384]{1,0:T(8,128)(2,1)} %constant.15.clone.refs_5_) | copy-start | bytes 589828
  32.5 22.1 %all-to-all-start = ((s16[8,272,256]{2,1,0:T(8,128)(2,1)}), s16[8,272,256]{2,1,0:T(8,128)(2,1)S(1)}, u32[]{:S(2)}, u32[]{:S(2)}) async-start(s16[8,272,256]{2,1,0:T(8,128)(2,1)} %exit_waves.1), calls=%async_computation | async-start | bytes 2228224 | tf_op jit(solution)/shard_map/all_to_all | solution.py:414
  54.7 0.9 copy-start.5
  72.6 16.7 %collective-permute-start.3 = (s16[8,144,256]{2,1,0:T(8,128)(2,1)S(1)}, s16[8,144,256]{2,1,0:T(8,128)(2,1)S(1)}, u32[]{:S(2)}, u32[]{:S(2)}) collective-permute-start(s16[8,144,256]{2,1,0:T(8,128)(2,1)S(1)} %get-tuple-element.5), channel_id=1, source_target_pairs={{1,0},{2,1},{3,2},{4,3},{5,4},{6,5},{7,6},{8,7},{9,8},{10,9},{11,1... | collective-permute-start | bytes 1769480 | tf_op jit(solution)/shard_map/ppermute | solution.py:358
  74.6 20.0 %collective-permute-start.2 = (s16[8,144,256]{2,1,0:T(8,128)(2,1)S(1)}, s16[8,144,256]{2,1,0:T(8,128)(2,1)S(1)}, u32[]{:S(2)}, u32[]{:S(2)}) collective-permute-start(s16[8,144,256]{2,1,0:T(8,128)(2,1)S(1)} %get-tuple-element.6), channel_id=1, source_target_pairs={{0,1},{1,2},{2,3},{3,4},{4,5},{5,6},{6,7},{7,8},{8,9},{9,10},{10,1... | collective-permute-start | bytes 1769480 | tf_op jit(solution)/shard_map/ppermute | solution.py:358
where the time goes:
time: 102 us; the launch traced here: 101 us
  waiting for transfers between devices  42 us (41%)
  Pallas kernels  20.5 us (20%)
  starting transfers between devices  19.8 us (19%)
  blocking collectives  14.7 us (14%)
  local copies, waits for them, and re-layouts  2.47 us (2%)
    ppermute x4, waiting for transfers between devices, passed_along(): lax.ppermute(value, 'lat', [(source, source + steps) for source in range(...  26.9 us
    all_to_all x1, waiting for transfers between devices, shards(): received = lax.all_to_all(partials, 'depth', 0, 0)  15.2 us
    all_gather x1, blocking collectives, shards(): gathered = lax.all_gather(back, 'depth')  14.7 us
    ppermute x4, starting transfers between devices, passed_along(): lax.ppermute(value, 'lat', [(source, source + steps) for source in range(...  13.5 us
    pallas_call x1, Pallas kernels, shards(): pl.pallas_call(lambda *refs: rim_kernel(*refs, total=total), out_shape=sh...  6.72 us
    all_to_all x1, starting transfers between devices, shards(): received = lax.all_to_all(partials, 'depth', 0, 0)  6.31 us
    pallas_call x1, Pallas kernels, shards(): pl.pallas_call(lambda *refs: exit_kernel(*refs, total=total), out_shape=j...  6.04 us
    pallas_call x1, Pallas kernels, shards(): pl.pallas_call(lambda *refs: own_kernel(*refs, total=total), out_shape=sh...  5.49 us
  transfers between devices with their start and end apart: 5, of which 5 were waited for; matrix products, arithmetic and copies ran while one was open for 0% of the time, Pallas kernels for 5%

commit v1 on v0

v1 whole, which is shorter than its diff:
```python
import math

import jax
import jax.numpy as jnp
import ml_dtypes
import numpy as np
from jax import lax
from jax.experimental import pallas as pl
from jax.experimental.pallas import tpu as pltpu
from jax.sharding import PartitionSpec as P

INTERPRET = False
PIECES = 1
LANES = 128
HEAD = 16
STEPS = 128.0
TOP = 32700.0
SHIFTER = 12582912.0


def split_pair(table):
    high = table.astype(ml_dtypes.bfloat16)
    low = (table - high.astype(np.float64)).astype(ml_dtypes.bfloat16)
    return high, low


def dft_pair(length):
    index = np.arange(length, dtype=np.int64)
    theta = 2.0 * np.pi / length * (index[:, None] * index[None, :] % length)
    factor = 1.0 / math.sqrt(length)
    return np.cos(theta) * factor, np.sin(theta) * factor


def row_table(length):
    high, low = split_pair(np.concatenate(dft_pair(length), axis=0))
    return np.concatenate([high, low, high], axis=1)


def column_tables(length):
    return split_pair(np.concatenate(dft_pair(length), axis=1))


def column_code(peak):
    bounded = jnp.maximum(peak, 2.0**-100)
    return jnp.ceil(jnp.log(bounded) * (STEPS / math.log(2.0))) + 1.0


def code_gain(code):
    return TOP * jnp.exp(code * (-math.log(2.0) / STEPS))


def code_step(code):
    return jnp.exp(code * (math.log(2.0) / STEPS)) * (1.0 / TOP)


def coded(value, gain):
    rounded = (value * gain + SHIFTER) - SHIFTER
    return rounded.astype(jnp.int32).astype(jnp.int16)


def widened(value):
    return value.astype(jnp.int32).astype(jnp.float32)


def shift_of(shear, level, total):
    return lax.shift_right_arithmetic(shear * (2 * level - total), int(math.log2(2 * total)))


def exit_kernel(
    slab, positions, angles, shears, cosines, sines, own, low, high, out, extended, wave, staged, sem
):
    frames = out.shape[0]
    levels, tile = own.shape[1], own.shape[2]
    reach = tile // 2
    halves = own.shape[3] // LANES
    total = 8 * levels
    first = slab[0] * levels

    def fill(level, carry):
        for part in range(2):
            rim = pl.ds((part * levels + level) * reach, reach)
            for half in range(halves):
                lanes = slice(half * LANES, (half + 1) * LANES)
                extended[part, level, half, :reach] = low[rim, lanes].astype(jnp.float32)
                extended[part, level, half, reach : reach + tile] = own[
                    part, level, :, lanes
                ].astype(jnp.float32)
                extended[part, level, half, reach + tile :] = high[rim, lanes].astype(jnp.float32)
        return carry

    lax.fori_loop(0, levels, fill, 0)

    def one(frame, carry):
        angle = angles[frame]
        shear = shears[angle]
        base = reach + positions[frame]
        starts = [base + shift_of(shear, first + level, total) for level in range(levels)]
        ramps = [
            (cosines[angle * levels + level], sines[angle * levels + level])
            for level in range(levels)
        ]
        for half in range(halves):
            lanes = slice(half * LANES, (half + 1) * LANES)
            peak = jnp.zeros((1, LANES), jnp.float32)
            for chunk in range(2):
                sum_real = jnp.zeros((reach, LANES), jnp.float32)
                sum_imag = jnp.zeros((reach, LANES), jnp.float32)
                for level in range(levels):
                    rows = pl.ds(starts[level] + chunk * reach, reach)
                    real = extended[0, level, half, rows]
                    imag = extended[1, level, half, rows]
                    ramp_real, ramp_imag = ramps[level]
                    sum_real = sum_real + (real * ramp_real - imag * ramp_imag)
                    sum_imag = sum_imag + (real * ramp_imag + imag * ramp_real)
                wave[0, chunk] = sum_real
                wave[1, chunk] = sum_imag
                top = jnp.maximum(jnp.abs(sum_real), jnp.abs(sum_imag))
                peak = jnp.maximum(peak, jnp.max(top, axis=0, keepdims=True))
            code = column_code(peak)
            gain = code_gain(code)
            for part in range(2):
                for chunk in range(2):
                    at = (part * 2 + chunk) * reach
                    staged[frame, at : at + reach, lanes] = coded(wave[part, chunk], gain)
            staged[frame, 4 * reach :, lanes] = (
                jnp.broadcast_to(code, (HEAD, LANES)).astype(jnp.int32).astype(jnp.int16)
            )
        pltpu.make_async_copy(staged.at[frame], out.at[frame], sem).start()
        return carry

    lax.fori_loop(0, frames, one, 0)
    pltpu.make_async_copy(staged, out, sem).wait()


def halves_of(value):
    high = value.astype(jnp.bfloat16)
    low = (value - high.astype(jnp.float32)).astype(jnp.bfloat16)
    return high, low


def matmul(left, right):
    return jnp.dot(left, right, preferred_element_type=jnp.float32)


def row_products(table, real, imag):
    high, low = halves_of(jnp.concatenate([real, imag], axis=1))
    both = matmul(table[...], jnp.concatenate([high, high, low], axis=0))
    rows, columns = real.shape
    return (
        both[:rows, :columns],
        both[:rows, columns:],
        both[rows:, :columns],
        both[rows:, columns:],
    )


def column_products(table_high, table_low, real, imag):
    high, low = halves_of(jnp.concatenate([real, imag], axis=0))
    both = matmul(high, table_high[...])
    both = both + matmul(high, table_low[...])
    both = both + matmul(low, table_high[...])
    rows, columns = real.shape
    return (
        both[:rows, :columns],
        both[rows:, :columns],
        both[:rows, columns:],
        both[rows:, columns:],
    )


def frame_kernel(
    slot,
    count,
    *refs,
    total,
):
    *parts, probe, intensity, row_ref, column_high, column_low, out, high_out, low_out = refs
    tile = probe.shape[1]
    reach = tile // 2
    sums_real, sums_imag = [], []
    for partials in parts:
        sum_real = jnp.zeros((tile, partials.shape[2]), jnp.float32)
        sum_imag = jnp.zeros((tile, partials.shape[2]), jnp.float32)
        for source in range(partials.shape[0]):
            step = code_step(widened(partials[source, 4 * reach :])[:1])
            sum_real = sum_real + widened(partials[source, : 2 * reach]) * step
            sum_imag = sum_imag + widened(partials[source, 2 * reach : 4 * reach]) * step
        sums_real.append(sum_real)
        sums_imag.append(sum_imag)
    sum_real = jnp.concatenate(sums_real, axis=1)
    sum_imag = jnp.concatenate(sums_imag, axis=1)
    scale = 1.0 / math.sqrt(total)
    sum_real = sum_real * scale
    sum_imag = sum_imag * scale
    probe_real = probe[0].astype(jnp.float32)
    probe_imag = probe[1].astype(jnp.float32)
    wave_real = probe_real * sum_real - probe_imag * sum_imag
    wave_imag = probe_real * sum_imag + probe_imag * sum_real

    cos_real, cos_imag, sin_real, sin_imag = row_products(row_ref, wave_real, wave_imag)
    mid_real = cos_real + sin_imag
    mid_imag = cos_imag - sin_real
    cos_real, cos_imag, sin_real, sin_imag = column_products(
        column_high, column_low, mid_real, mid_imag
    )
    far_real = cos_real + sin_imag
    far_imag = cos_imag - sin_real

    magnitude = jnp.sqrt(far_real * far_real + far_imag * far_imag)
    amplitude = jnp.sqrt(intensity[0].astype(jnp.float32))
    valid = jnp.where(slot[0] < count[0], 1.0, 0.0).astype(jnp.float32)
    factor = (amplitude / jnp.maximum(magnitude, 0.5) - 1.0) * valid
    far_real = far_real * factor
    far_imag = far_imag * factor

    cos_real, cos_imag, sin_real, sin_imag = column_products(
        column_high, column_low, far_real, far_imag
    )
    mid_real = cos_real - sin_imag
    mid_imag = cos_imag + sin_real
    cos_real, cos_imag, sin_real, sin_imag = row_products(row_ref, mid_real, mid_imag)
    update_real = cos_real - sin_imag
    update_imag = cos_imag + sin_real

    back_real = probe_real * update_real + probe_imag * update_imag
    back_imag = probe_real * update_imag - probe_imag * update_real
    peak = jnp.max(
        jnp.maximum(jnp.abs(back_real), jnp.abs(back_imag)), axis=0, keepdims=True
    )
    code = column_code(peak)
    gain = code_gain(code)
    coded_real = coded(back_real, gain)
    coded_imag = coded(back_imag, gain)
    head = jnp.broadcast_to(code, (HEAD, code.shape[1])).astype(jnp.int32).astype(jnp.int16)
    out[: 2 * reach] = coded_real
    out[2 * reach : 4 * reach] = coded_imag
    out[4 * reach :] = head
    low_out[:reach] = coded_real[:reach]
    low_out[reach : 2 * reach] = coded_imag[:reach]
    low_out[2 * reach :] = head
    high_out[:reach] = coded_real[reach:]
    high_out[reach : 2 * reach] = coded_imag[reach:]
    high_out[2 * reach :] = head


def correction_kernel(
    slab, positions, angles, below, above, shears, cosines, sines, *refs
):
    mine, theirs, out, inner, rims, staged, sem = refs
    levels, tile = out.shape[1], out.shape[2]
    reach = tile // 2
    halves = out.shape[3] // LANES
    share = mine.shape[0]
    frames = 2 * share
    total = 8 * levels
    blank = jnp.zeros((reach, LANES), jnp.float32)
    bottom, top = 4 * reach + HEAD, 6 * reach + 2 * HEAD

    for source, odd in ((mine, slab[0] & 1), (theirs, 1 - (slab[0] & 1))):

        def fill(item, carry, source=source, odd=odd):
            frame = 2 * item + odd
            for half in range(halves):
                lanes = slice(half * LANES, (half + 1) * LANES)

                def step_at(row):
                    return code_step(widened(source[item, row : row + HEAD, lanes])[:1])

                step = step_at(4 * reach)
                low_step = step_at(bottom + 2 * reach)
                high_step = step_at(top + 2 * reach)
                for part in range(2):
                    inner[part, frame, half, :reach] = blank
                    at = 2 * part * reach
                    inner[part, frame, half, reach : reach + tile] = (
                        widened(source[item, at : at + tile, lanes]) * step
                    )
                    inner[part, frame, half, reach + tile :] = blank
                    at = bottom + part * reach
                    rims[0, part, frame, half, :reach] = (
                        widened(source[item, at : at + reach, lanes]) * low_step
                    )
                    rims[0, part, frame, half, reach:] = blank
                    at = top + part * reach
                    rims[1, part, frame, half, :reach] = blank
                    rims[1, part, frame, half, reach:] = (
                        widened(source[item, at : at + reach, lanes]) * high_step
                    )
            return carry

        lax.fori_loop(0, share, fill, 0)

    def one(level, carry):
        here = slab[0] * levels + level
        starts, ramps = [], []
        for frame in range(frames):
            angle = angles[frame]
            starts.append(reach - positions[frame] - shift_of(shears[angle], here, total))
            ramps.append((cosines[angle * levels + level], sines[angle * levels + level]))
        for chunk, around in enumerate((below, above)):
            rim_starts, rim_ramps = [], []
            for frame in range(frames):
                angle = around[frames + frame]
                start = around[frame] + shift_of(shears[angle], here, total)
                if chunk == 0:
                    rim_starts.append(reach - jnp.maximum(start, 0))
                else:
                    rim_starts.append(-jnp.minimum(start, 0))
                rim_ramps.append((cosines[angle * levels + level], sines[angle * levels + level]))
            at = slice(chunk * reach, (chunk + 1) * reach)
            for half in range(halves):
                lanes = slice(half * LANES, (half + 1) * LANES)
                sum_real = jnp.zeros((reach, LANES), jnp.float32)
                sum_imag = jnp.zeros((reach, LANES), jnp.float32)
                for frame in range(frames):
                    rows = pl.ds(starts[frame] + chunk * reach, reach)
                    rim_rows = pl.ds(rim_starts[frame], reach)
                    for real, imag, (ramp_real, ramp_imag) in (
                        (inner[0, frame, half, rows], inner[1, frame, half, rows], ramps[frame]),
                        (
                            rims[chunk, 0, frame, half, rim_rows],
                            rims[chunk, 1, frame, half, rim_rows],
                            rim_ramps[frame],
                        ),
                    ):
                        sum_real = sum_real + (real * ramp_real + imag * ramp_imag)
                        sum_imag = sum_imag + (imag * ramp_real - real * ramp_imag)
                staged[0, level, at, lanes] = sum_real
                staged[1, level, at, lanes] = sum_imag
        for part in range(2):
            pltpu.make_async_copy(staged.at[part, level], out.at[part, level], sem).start()
        return carry

    lax.fori_loop(0, levels, one, 0)
    pltpu.make_async_copy(staged, out, sem).wait()


def scalars():
    return pl.BlockSpec(memory_space=pltpu.SMEM)


def resident(shape):
    return pl.BlockSpec(shape, lambda *_: (0,) * len(shape), pipeline_mode=pl.Buffered(1))


def params(mebibytes):
    return pltpu.CompilerParams(vmem_limit_bytes=mebibytes << 20)


def passed_along(value, steps):
    count = lax.axis_size("lat")
    initial, last = (max(0, -steps), min(count, count - steps))
    return lax.ppermute(value, "lat", [(source, source + steps) for source in range(initial, last)])


def shards(
    object_field,
    probe_field,
    intensity,
    depth_phase,
    shear_rate,
    positions,
    angle_index,
    frame_count,
):
    levels = object_field.shape[1]
    tile = object_field.shape[2]
    width = object_field.shape[3]
    frames = positions.shape[0]
    reach = tile // 2
    halves = width // LANES
    slabs = lax.axis_size("depth")
    total = levels * slabs
    slab = lax.axis_index("depth").astype(jnp.int32).reshape(1)
    coded_rows = 2 * tile + HEAD

    spots = jnp.concatenate([positions, angle_index]).astype(jnp.bfloat16)
    spots = jnp.pad(spots[None], ((0, HEAD - 1), (0, width - 2 * frames)))
    rim_rows = 2 * levels * reach
    last = object_field[:, :, reach:].reshape(rim_rows, width)
    start = object_field[:, :, :reach].reshape(rim_rows, width)
    span = width // PIECES
    rims = []
    for piece in range(PIECES):
        lanes = slice(piece * span, (piece + 1) * span)
        pair = [last[:, lanes], start[:, lanes]]
        if piece == 0:
            pair = [jnp.concatenate([rows, spots[:, lanes]]) for rows in pair]
        rims.append((passed_along(pair[0], 1), passed_along(pair[1], -1)))
    below = rims[0][0][rim_rows, : 2 * frames].astype(jnp.int32)
    above = rims[0][1][rim_rows, : 2 * frames].astype(jnp.int32)
    cosines = jnp.cos(depth_phase).reshape(-1)
    sines = jnp.sin(depth_phase).reshape(-1)

    received = []
    for piece, (low, high) in enumerate(rims):
        block = (2, levels, tile, span)
        partials = pl.pallas_call(
            exit_kernel,
            out_shape=jax.ShapeDtypeStruct((frames, coded_rows, span), jnp.int16),
            grid=(1,),
            in_specs=[scalars()] * 6
            + [
                pl.BlockSpec(
                    block, lambda _, p=piece: (0, 0, 0, p), pipeline_mode=pl.Buffered(1)
                ),
                resident(low.shape),
                resident(high.shape),
            ],
            out_specs=pl.BlockSpec(memory_space=pl.ANY),
            scratch_shapes=[
                pltpu.VMEM((2, levels, span // LANES, 2 * tile, LANES), jnp.float32),
                pltpu.VMEM((2, 2, reach, LANES), jnp.float32),
                pltpu.VMEM((frames, coded_rows, span), jnp.int16),
                pltpu.SemaphoreType.DMA(()),
            ],
            compiler_params=params(16),
            interpret=INTERPRET,
            name=f"exit_waves_{piece}",
        )(slab, positions, angle_index, shear_rate, cosines, sines, object_field, low, high)
        received.append(lax.all_to_all(partials, "depth", 0, 0))

    table = jnp.asarray(row_table(tile))
    column_high, column_low = (jnp.asarray(t) for t in column_tables(width))
    half_rows = tile + HEAD
    back, to_above, to_below = pl.pallas_call(
        lambda *refs: frame_kernel(*refs, total=total),
        out_shape=[
            jax.ShapeDtypeStruct((rows, width), jnp.int16)
            for rows in (coded_rows, half_rows, half_rows)
        ],
        grid_spec=pltpu.PrefetchScalarGridSpec(
            num_scalar_prefetch=2,
            grid=(1,),
            in_specs=[resident(part.shape) for part in received]
            + [
                resident(probe_field.shape),
                pl.BlockSpec((1, tile, width), lambda i, slot, count: (slot[0], 0, 0)),
                resident(table.shape),
                resident(column_high.shape),
                resident(column_low.shape),
            ],
            out_specs=[
                pl.BlockSpec((rows, width), lambda *_: (0, 0))
                for rows in (coded_rows, half_rows, half_rows)
            ],
        ),
        compiler_params=params(16),
        interpret=INTERPRET,
        name="far_field",
    )(slab, frame_count, *received, probe_field, intensity, table, column_high, column_low)

    bundle = jnp.concatenate([back, passed_along(to_above, 1), passed_along(to_below, -1)])
    lanes_of = [[d for d in range(slabs) if d % 2 == core] for core in range(2)]
    mine = lax.all_gather(bundle, "depth", axis_index_groups=lanes_of)
    theirs = lax.ppermute(mine, "depth", [(d, d ^ 1) for d in range(slabs)])

    return pl.pallas_call(
        correction_kernel,
        out_shape=jax.ShapeDtypeStruct((2, levels, tile, width), jnp.float32),
        grid=(1,),
        in_specs=[scalars()] * 8 + [resident(mine.shape), resident(theirs.shape)],
        out_specs=pl.BlockSpec(memory_space=pl.ANY),
        scratch_shapes=[
            pltpu.VMEM((2, frames, halves, 2 * tile, LANES), jnp.float32),
            pltpu.VMEM((2, 2, frames, halves, tile, LANES), jnp.float32),
            pltpu.VMEM((2, levels, tile, width), jnp.float32),
            pltpu.SemaphoreType.DMA(()),
        ],
        compiler_params=params(24),
        interpret=INTERPRET,
        name="corrections",
    )(slab, positions, angle_index, below, above, shear_rate, cosines, sines, mine, theirs)


def solution(mesh):
    placed = (
        P(None, "depth", "lat", None),
        P(),
        P("lat", None, None),
        P(None, "depth"),
        P(),
        P("lat"),
        P("lat"),
        P("lat"),
    )
    return jax.shard_map(
        shards, mesh=mesh, in_specs=placed, out_specs=P(None, "depth", "lat", None), check_vma=False
    )
```

time: 102 us -> 97.8 us (0.959)
  the two profiles are of different devices: /device:TPU:385 before, /device:TPU:249 now
where the time goes in v1:
time: 97.8 us; the launch traced here: 97.5 us
  waiting for transfers between devices  34 us (35%)
  starting transfers between devices  30.2 us (31%)
  Pallas kernels  16.8 us (17%)
  blocking collectives  13.6 us (14%)
  local copies, waits for them, and re-layouts  1.79 us (2%)
    ppermute x4, starting transfers between devices, passed_along(): lax.ppermute(value, 'lat', [(source, source + steps) for source in range(...  18.2 us
    ppermute x4, waiting for transfers between devices, passed_along(): lax.ppermute(value, 'lat', [(source, source + steps) for source in range(...  16.5 us
    all_to_all x1, waiting for transfers between devices, shards(): received.append(lax.all_to_all(partials, 'depth', 0, 0))  15.2 us
    all_gather x1, blocking collectives, shards(): mine = lax.all_gather(bundle, 'depth', axis_index_groups=lanes_of)  13.6 us
    pallas_call x1, Pallas kernels, shards(): pl.pallas_call(correction_kernel, out_shape=jax.ShapeDtypeStruct((2, leve...  9.95 us
    all_to_all x1, starting transfers between devices, shards(): received.append(lax.all_to_all(partials, 'depth', 0, 0))  6.3 us
    ppermute x1, starting transfers between devices, shards(): theirs = lax.ppermute(mine, 'depth', [(d, d ^ 1) for d in range(slabs)])  5.7 us
    pallas_call x1, Pallas kernels, shards(): pl.pallas_call(exit_kernel, out_shape=jax.ShapeDtypeStruct((frames, coded...  4.61 us
  transfers between devices with their start and end apart: 6, of which 5 were waited for; matrix products, arithmetic and copies ran while one was open for 0% of the time, Pallas kernels for 0%

profile of v1, /device:TPU:249, one launch (start us, length us, event | category | flops | bytes accessed | tf_op | source)
XLA Modules:
  0.0 97.5 jit_solution(6633756858595511968)
XLA Ops:
  0.0 1.3 %fusion.8 = (bf16[2,8,64,256]{3,2,1,0:T(8,128)(2,1)S(1)}, bf16[2,8,64,256]{3,2,1,0:T(8,128)(2,1)S(1)}) fusion(bf16[2,8,128,256]{3,2,1,0:T(8,128)(2,1)} %own.1), kind=kLoop, calls=%fused_computation.17 | loop fusion | bytes 2097152 | tf_op jit(solution)/shard_map/slice | solution.py:381
  1.4 0.0 copy-start.16
  1.4 0.1 fusion.5
  1.5 0.1 pad_maximum_fusion
  1.5 2.5 %collective-permute-start.1 = (bf16[1040,256]{1,0:T(8,128)(2,1)S(1)}, bf16[1040,256]{1,0:T(8,128)(2,1)S(1)}, u32[]{:S(2)}, u32[]{:S(2)}) collective-permute-start(bf16[1040,256]{1,0:T(8,128)(2,1)S(1)} %get-tuple-element.13), channel_id=1, source_target_pairs={{1,0},{2,1},{3,2},{4,3},{5,4},{6,5},{7,6},{8,7},{9,8},{10,9},{11,1... | collective-permute-start | bytes 1597448 | tf_op jit(solution)/shard_map/ppermute | solution.py:353
  4.1 6.2 %collective-permute-start = (bf16[1040,256]{1,0:T(8,128)(2,1)S(1)}, bf16[1040,256]{1,0:T(8,128)(2,1)S(1)}, u32[]{:S(2)}, u32[]{:S(2)}) collective-permute-start(bf16[1040,256]{1,0:T(8,128)(2,1)S(1)} %get-tuple-element.14), channel_id=1, source_target_pairs={{0,1},{1,2},{2,3},{3,4},{4,5},{5,6},{6,7},{7,8},{8,9},{9,10},{10,1... | collective-permute-start | bytes 1597448 | tf_op jit(solution)/shard_map/ppermute | solution.py:353
  10.3 0.1 copy.13
  10.4 0.1 reshape.54.sines
  10.5 0.1 copy.12
  10.6 0.1 reshape.53.cosines
  10.7 9.1 %collective-permute-done.1.high = bf16[1040,256]{1,0:T(8,128)(2,1)S(1)} collective-permute-done((bf16[1040,256]{1,0:T(8,128)(2,1)S(1)}, bf16[1040,256]{1,0:T(8,128)(2,1)S(1)}, u32[]{:S(2)}, u32[]{:S(2)}) %collective-permute-start.1) | collective-permute-done | bytes 532512 | tf_op jit(solution)/shard_map/ppermute | solution.py:353
  19.9 0.9 collective-permute-done.low
  20.7 4.6 %exit_waves_0.1 = s16[8,272,256]{2,1,0:T(8,128)(2,1)} custom-call(s32[1]{0:T(128)} %bitcast.slab.refs_0_, s32[8]{0:T(128)S(1)} %copy-done.10, s32[8]{0:T(128)S(1)} %copy-done.12, s32[32]{0:T(128)S(1)} %copy-done.14, f32[256]{0:T(256)S(1)} %reshape.53.cosines, f32[256]{0:T(256)S(1)} %reshape.54.sines, bf16[2,8,128,256]{3,2,1,0:T(8,128)(2,1)S(1)} %copy-done, ...), custom_call_target="tpu_custom_call" | custom-call | tf_op jit(solution)/shard_map/exit_waves_0/pallas_call | solution.py:398
  25.4 0.0 copy-start.1
  25.4 0.0 copy-start.2
  25.4 0.0 copy-start.3
  25.4 0.0 copy-start.4
  25.4 0.0 copy-start.5
  25.4 6.3 %all-to-all-start = ((s16[8,272,256]{2,1,0:T(8,128)(2,1)}), s16[8,272,256]{2,1,0:T(8,128)(2,1)S(1)}, u32[]{:S(2)}, u32[]{:S(2)}) async-start(s16[8,272,256]{2,1,0:T(8,128)(2,1)} %exit_waves_0.1), calls=%async_computation | async-start | bytes 2228224 | tf_op jit(solution)/shard_map/all_to_all | solution.py:421
  32.4 15.2 %all-to-all-done.refs_2_ = s16[8,272,256]{2,1,0:T(8,128)(2,1)S(1)} async-done(((s16[8,272,256]{2,1,0:T(8,128)(2,1)}), s16[8,272,256]{2,1,0:T(8,128)(2,1)S(1)}, u32[]{:S(2)}, u32[]{:S(2)}) %all-to-all-start) | async-done | bytes 1114144 | tf_op jit(solution)/shard_map/all_to_all | solution.py:421
  47.6 2.3 %far_field.1 = (s16[272,256]{1,0:T(8,128)(2,1)S(1)}, s16[144,256]{1,0:T(8,128)(2,1)S(1)}, s16[144,256]{1,0:T(8,128)(2,1)S(1)}) custom-call(s32[1]{0:T(128)} %bitcast.slab.refs_0_, s32[1]{0:T(128)S(6)} %copy.14.refs_1_, s16[8,272,256]{2,1,0:T(8,128)(2,1)S(1)} %all-to-all-done.refs_2_, bf16[2,128,256]{2,1,0:T(8,128)(2,1)S(1)} %copy-done.5, ...), custom_call_target="tpu_custom_call" | custom-call | tf_op jit(solution)/shard_map/far_field/pallas_call | solution.py:426
  49.8 0.0 copy-start.11
  49.8 0.0 copy-start.13
  49.9 0.0 copy-start.15
  49.9 7.6 %collective-permute-start.2 = (s16[144,256]{1,0:T(8,128)(2,1)S(1)}, s16[144,256]{1,0:T(8,128)(2,1)S(1)}, u32[]{:S(2)}, u32[]{:S(2)}) collective-permute-start(s16[144,256]{1,0:T(8,128)(2,1)S(1)} %get-tuple-element.9), channel_id=1, source_target_pairs={{0,1},{1,2},{2,3},{3,4},{4,5},{5,6},{6,7},{7,8},{8,9},{9,10},{10,1... | collective-permute-start | bytes 221192 | tf_op jit(solution)/shard_map/ppermute | solution.py:353
  57.4 1.9 %collective-permute-start.3 = (s16[144,256]{1,0:T(8,128)(2,1)S(1)}, s16[144,256]{1,0:T(8,128)(2,1)S(1)}, u32[]{:S(2)}, u32[]{:S(2)}) collective-permute-start(s16[144,256]{1,0:T(8,128)(2,1)S(1)} %get-tuple-element.10), channel_id=1, source_target_pairs={{1,0},{2,1},{3,2},{4,3},{5,4},{6,5},{7,6},{8,7},{9,8},{10,9},{11,1... | collective-permute-start | bytes 221192 | tf_op jit(solution)/shard_map/ppermute | solution.py:353
  59.4 0.0 collective-permute-done.2
  59.4 6.5 %collective-permute-done.3 = s16[144,256]{1,0:T(8,128)(2,1)S(1)} collective-permute-done((s16[144,256]{1,0:T(8,128)(2,1)S(1)}, s16[144,256]{1,0:T(8,128)(2,1)S(1)}, u32[]{:S(2)}, u32[]{:S(2)}) %collective-permute-start.3) | collective-permute-done | bytes 73760 | tf_op jit(solution)/shard_map/ppermute | solution.py:353
  65.9 13.6 %all-gather.2 = s16[2240,256]{1,0:T(8,128)(2,1)S(1)} all-gather(s16[560,256]{1,0:T(8,128)(2,1)S(1)} %pad_add_fusion), channel_id=2, replica_groups={{0,128,256,384},{64,192,320,448},{1,129,257,385},{65,193,321,449},{2,13..., dimensions={0}, use_global_device_ids=true | all-gather | bytes 1433600 | tf_op jit(solution)/shard_map/all_gather | solution.py:455
  79.4 5.7 %collective-permute-start.4 = (s16[4,560,256]{2,1,0:T(8,128)(2,1)S(1)}, s16[4,560,256]{2,1,0:T(8,128)(2,1)S(1)}, u32[]{:S(2)}, u32[]{:S(2)}) collective-permute-start(s16[4,560,256]{2,1,0:T(8,128)(2,1)S(1)} %bitcast.18), channel_id=1, source_target_pairs={{0,64},{64,0},{128,192},{192,128},{256,320},{320,256},{384,448},{4... | collective-permute-start | bytes 3440648 | tf_op jit(solution)/shard_map/ppermute | solution.py:456
  85.2 2.4 %collective-permute-done.4.refs_1_ = s16[4,560,256]{2,1,0:T(8,128)(2,1)S(1)} collective-permute-done((s16[4,560,256]{2,1,0:T(8,128)(2,1)S(1)}, s16[4,560,256]{2,1,0:T(8,128)(2,1)S(1)}, u32[]{:S(2)}, u32[]{:S(2)}) %collective-permute-start.4) | collective-permute-done | bytes 1146912 | tf_op jit(solution)/shard_map/ppermute | solution.py:456
  87.6 9.9 %corrections.1 = f32[2,8,128,256]{3,2,1,0:T(8,128)} custom-call(s32[1]{0:T(128)} %bitcast.slab.refs_0_, s32[8]{0:T(128)S(1)} %copy-done.11, s32[8]{0:T(128)S(1)} %copy-done.13, s32[16]{0:T(128)S(1)} %fusion.7.below, s32[16]{0:T(128)S(1)} %fusion.6.above, s32[32]{0:T(128)S(1)} %copy-done.15, f32[256]{0:T(256)S(1)} %copy-done.9, f32[256]{0:T(256)S(1)} %copy-done.7, ...), custom_call_target="tpu_custom_call" | custom-call | tf_op jit(solution)/shard_map/corrections/pallas_call | solution.py:458
  (30 shorter events, 0.1 us)
Async XLA Ops:
  0.0 1.3 %copy-start.12 = (s32[8]{0:T(128)S(1)}, s32[8]{0:T(128)}, u32[]{:S(2)}) copy-start(s32[8]{0:T(128)} %angles.3) | copy-start | bytes 100
  0.0 1.3 %copy-start.10 = (s32[8]{0:T(128)S(1)}, s32[8]{0:T(128)}, u32[]{:S(2)}) copy-start(s32[8]{0:T(128)} %positions.3) | copy-start | bytes 100
  1.4 8.9 %copy-start.16 = (f32[32,8]{0,1:T(8,128)S(1)}, f32[32,8]{0,1:T(8,128)}, u32[]{:S(2)}) copy-start(f32[32,8]{0,1:T(8,128)} %param.14) | copy-start | bytes 3076
  1.5 19.3 %copy-start = (bf16[2,8,128,256]{3,2,1,0:T(8,128)(2,1)S(1)}, bf16[2,8,128,256]{3,2,1,0:T(8,128)(2,1)}, u32[]{:S(2)}) copy-start(bf16[2,8,128,256]{3,2,1,0:T(8,128)(2,1)} %own.1) | copy-start | bytes 3145732
  1.5 19.3 %copy-start.14 = (s32[32]{0:T(128)S(1)}, s32[32]{0:T(128)}, u32[]{:S(2)}) copy-start(s32[32]{0:T(128)} %shears.3) | copy-start | bytes 388
  1.5 18.3 %collective-permute-start.1 = (bf16[1040,256]{1,0:T(8,128)(2,1)S(1)}, bf16[1040,256]{1,0:T(8,128)(2,1)S(1)}, u32[]{:S(2)}, u32[]{:S(2)}) collective-permute-start(bf16[1040,256]{1,0:T(8,128)(2,1)S(1)} %get-tuple-element.13), channel_id=1, source_target_pairs={{1,0},{2,1},{3,2},{4,3},{5,4},{6,5},{7,6},{8,7},{9,8},{10,9},{11,1... | collective-permute-start | bytes 1597448 | tf_op jit(solution)/shard_map/ppermute | solution.py:353
  4.1 16.7 %collective-permute-start = (bf16[1040,256]{1,0:T(8,128)(2,1)S(1)}, bf16[1040,256]{1,0:T(8,128)(2,1)S(1)}, u32[]{:S(2)}, u32[]{:S(2)}) collective-permute-start(bf16[1040,256]{1,0:T(8,128)(2,1)S(1)} %get-tuple-element.14), channel_id=1, source_target_pairs={{0,1},{1,2},{2,3},{3,4},{4,5},{5,6},{6,7},{7,8},{8,9},{9,10},{10,1... | collective-permute-start | bytes 1597448 | tf_op jit(solution)/shard_map/ppermute | solution.py:353
  10.5 14.8 %copy-start.6 = (f32[256]{0:T(256)}, f32[256]{0:T(256)S(1)}, u32[]{:S(2)}) copy-start(f32[256]{0:T(256)S(1)} %reshape.54.sines) | copy-start | bytes 3076
  10.7 14.7 %copy-start.8 = (f32[256]{0:T(256)}, f32[256]{0:T(256)S(1)}, u32[]{:S(2)}) copy-start(f32[256]{0:T(256)S(1)} %reshape.53.cosines) | copy-start | bytes 3076
  25.4 22.2 %copy-start.1 = (bf16[8,128,256]{2,1,0:T(8,128)(2,1)S(1)}, bf16[8,128,256]{2,1,0:T(8,128)(2,1)}, u32[]{:S(2)}) copy-start(bf16[8,128,256]{2,1,0:T(8,128)(2,1)} %refs_4_.1) | copy-start | bytes 1572868
  25.4 22.2 %copy-start.2 = (bf16[256,512]{1,0:T(8,128)(2,1)S(1)}, bf16[256,512]{1,0:T(8,128)(2,1)}, u32[]{:S(2)}) copy-start(bf16[256,512]{1,0:T(8,128)(2,1)} %constant.17.clone.refs_7_) | copy-start | bytes 786436
  25.4 22.1 %copy-start.3 = (bf16[256,512]{1,0:T(8,128)(2,1)S(1)}, bf16[256,512]{1,0:T(8,128)(2,1)}, u32[]{:S(2)}) copy-start(bf16[256,512]{1,0:T(8,128)(2,1)} %constant.16.clone.refs_6_) | copy-start | bytes 786436
  25.4 22.1 %copy-start.4 = (bf16[256,384]{1,0:T(8,128)(2,1)S(1)}, bf16[256,384]{1,0:T(8,128)(2,1)}, u32[]{:S(2)}) copy-start(bf16[256,384]{1,0:T(8,128)(2,1)} %constant.15.clone.refs_5_) | copy-start | bytes 589828
  25.4 22.1 %copy-start.5 = (bf16[2,128,256]{2,1,0:T(8,128)(2,1)S(1)}, bf16[2,128,256]{2,1,0:T(8,128)(2,1)}, u32[]{:S(2)}) copy-start(bf16[2,128,256]{2,1,0:T(8,128)(2,1)} %refs_3_.1) | copy-start | bytes 393220
  25.4 22.1 %all-to-all-start = ((s16[8,272,256]{2,1,0:T(8,128)(2,1)}), s16[8,272,256]{2,1,0:T(8,128)(2,1)S(1)}, u32[]{:S(2)}, u32[]{:S(2)}) async-start(s16[8,272,256]{2,1,0:T(8,128)(2,1)} %exit_waves_0.1), calls=%async_computation | async-start | bytes 2228224 | tf_op jit(solution)/shard_map/all_to_all | solution.py:421
  49.8 37.7 %copy-start.7 = (f32[256]{0:T(256)S(1)}, f32[256]{0:T(256)}, u32[]{:S(2)}) copy-start(f32[256]{0:T(256)} %copy-done.6) | copy-start | bytes 3076
  49.8 37.7 %copy-start.9 = (f32[256]{0:T(256)S(1)}, f32[256]{0:T(256)}, u32[]{:S(2)}) copy-start(f32[256]{0:T(256)} %copy-done.8) | copy-start | bytes 3076
  49.8 37.7 %copy-start.11 = (s32[8]{0:T(128)S(1)}, s32[8]{0:T(128)}, u32[]{:S(2)}) copy-start(s32[8]{0:T(128)} %positions.3) | copy-start | bytes 100
  49.8 37.7 %copy-start.13 = (s32[8]{0:T(128)S(1)}, s32[8]{0:T(128)}, u32[]{:S(2)}) copy-start(s32[8]{0:T(128)} %angles.3) | copy-start | bytes 100
  49.9 37.7 %copy-start.15 = (s32[32]{0:T(128)S(1)}, s32[32]{0:T(128)}, u32[]{:S(2)}) copy-start(s32[32]{0:T(128)} %shears.3) | copy-start | bytes 388
  49.9 9.5 %collective-permute-start.2 = (s16[144,256]{1,0:T(8,128)(2,1)S(1)}, s16[144,256]{1,0:T(8,128)(2,1)S(1)}, u32[]{:S(2)}, u32[]{:S(2)}) collective-permute-start(s16[144,256]{1,0:T(8,128)(2,1)S(1)} %get-tuple-element.9), channel_id=1, source_target_pairs={{0,1},{1,2},{2,3},{3,4},{4,5},{5,6},{6,7},{7,8},{8,9},{9,10},{10,1... | collective-permute-start | bytes 221192 | tf_op jit(solution)/shard_map/ppermute | solution.py:353
  57.4 8.4 %collective-permute-start.3 = (s16[144,256]{1,0:T(8,128)(2,1)S(1)}, s16[144,256]{1,0:T(8,128)(2,1)S(1)}, u32[]{:S(2)}, u32[]{:S(2)}) collective-permute-start(s16[144,256]{1,0:T(8,128)(2,1)S(1)} %get-tuple-element.10), channel_id=1, source_target_pairs={{1,0},{2,1},{3,2},{4,3},{5,4},{6,5},{7,6},{8,7},{9,8},{10,9},{11,1... | collective-permute-start | bytes 221192 | tf_op jit(solution)/shard_map/ppermute | solution.py:353
  79.4 8.1 %collective-permute-start.4 = (s16[4,560,256]{2,1,0:T(8,128)(2,1)S(1)}, s16[4,560,256]{2,1,0:T(8,128)(2,1)S(1)}, u32[]{:S(2)}, u32[]{:S(2)}) collective-permute-start(s16[4,560,256]{2,1,0:T(8,128)(2,1)S(1)} %bitcast.18), channel_id=1, source_target_pairs={{0,64},{64,0},{128,192},{192,128},{256,320},{320,256},{384,448},{4... | collective-permute-start | bytes 3440648 | tf_op jit(solution)/shard_map/ppermute | solution.py:456

commit v2 on v1

--- a/solution.py
+++ b/solution.py
@@ -10,7 +10,6 @@
 from jax.sharding import PartitionSpec as P
 
 INTERPRET = False
-PIECES = 1
 LANES = 128
 HEAD = 16
 STEPS = 128.0
@@ -67,25 +66,31 @@
 
 
 def exit_kernel(
-    slab, positions, angles, shears, cosines, sines, own, low, high, out, extended, wave, staged, sem
+    place, positions, angles, shears, cosines, sines, own, near, far, out, extended, wave, staged, sem
 ):
     frames = out.shape[0]
     levels, tile = own.shape[1], own.shape[2]
     reach = tile // 2
     halves = own.shape[3] // LANES
     total = 8 * levels
-    first = slab[0] * levels
+    first = place[0] * levels
+    near_at = pl.multiple_of((1 - place[1]) * (reach + tile), reach)
+    far_at = pl.multiple_of(place[1] * (reach + tile), reach)
 
     def fill(level, carry):
         for part in range(2):
-            rim = pl.ds((part * levels + level) * reach, reach)
+            rim = pl.ds(pl.multiple_of((part * levels + level) * reach, reach), reach)
             for half in range(halves):
                 lanes = slice(half * LANES, (half + 1) * LANES)
-                extended[part, level, half, :reach] = low[rim, lanes].astype(jnp.float32)
+                extended[part, level, half, pl.ds(near_at, reach)] = near[rim, lanes].astype(
+                    jnp.float32
+                )
                 extended[part, level, half, reach : reach + tile] = own[
                     part, level, :, lanes
                 ].astype(jnp.float32)
-                extended[part, level, half, reach + tile :] = high[rim, lanes].astype(jnp.float32)
+                extended[part, level, half, pl.ds(far_at, reach)] = far[rim, lanes].astype(
+                    jnp.float32
+                )
         return carry
 
     lax.fori_loop(0, levels, fill, 0)
@@ -169,12 +174,12 @@
 
 
 def frame_kernel(
-    slot,
+    place,
     count,
     *refs,
     total,
 ):
-    *parts, probe, intensity, row_ref, column_high, column_low, out, high_out, low_out = refs
+    *parts, probe, intensity, row_ref, column_high, column_low, out, near_out, far_out = refs
     tile = probe.shape[1]
     reach = tile // 2
     sums_real, sums_imag = [], []
@@ -207,8 +212,8 @@
     far_imag = cos_imag - sin_real
 
     magnitude = jnp.sqrt(far_real * far_real + far_imag * far_imag)
-    amplitude = jnp.sqrt(intensity[0].astype(jnp.float32))
-    valid = jnp.where(slot[0] < count[0], 1.0, 0.0).astype(jnp.float32)
+    amplitude = jnp.sqrt(intensity[place[0]].astype(jnp.float32))
+    valid = jnp.where(place[0] < count[0], 1.0, 0.0).astype(jnp.float32)
     factor = (amplitude / jnp.maximum(magnitude, 0.5) - 1.0) * valid
     far_real = far_real * factor
     far_imag = far_imag * factor
@@ -235,67 +240,79 @@
     out[: 2 * reach] = coded_real
     out[2 * reach : 4 * reach] = coded_imag
     out[4 * reach :] = head
-    low_out[:reach] = coded_real[:reach]
-    low_out[reach : 2 * reach] = coded_imag[:reach]
-    low_out[2 * reach :] = head
-    high_out[:reach] = coded_real[reach:]
-    high_out[reach : 2 * reach] = coded_imag[reach:]
-    high_out[2 * reach :] = head
-
-
-def correction_kernel(
-    slab, positions, angles, below, above, shears, cosines, sines, *refs
-):
-    mine, theirs, out, inner, rims, staged, sem = refs
+
+    def rims(first_out, last_out):
+        first_out[:reach] = coded_real[:reach]
+        first_out[reach : 2 * reach] = coded_imag[:reach]
+        first_out[2 * reach :] = head
+        last_out[:reach] = coded_real[reach:]
+        last_out[reach : 2 * reach] = coded_imag[reach:]
+        last_out[2 * reach :] = head
+
+    @pl.when(place[1] == 0)
+    def _():
+        rims(far_out, near_out)
+
+    @pl.when(place[1] == 1)
+    def _():
+        rims(near_out, far_out)
+
+
+def correction_kernel(place, positions, angles, below, above, shears, cosines, sines, *refs):
+    gathered, out, inner, rims, staged, sem = refs
     levels, tile = out.shape[1], out.shape[2]
     reach = tile // 2
     halves = out.shape[3] // LANES
-    share = mine.shape[0]
-    frames = 2 * share
+    frames = gathered.shape[0]
     total = 8 * levels
     blank = jnp.zeros((reach, LANES), jnp.float32)
-    bottom, top = 4 * reach + HEAD, 6 * reach + 2 * HEAD
-
-    for source, odd in ((mine, slab[0] & 1), (theirs, 1 - (slab[0] & 1))):
-
-        def fill(item, carry, source=source, odd=odd):
-            frame = 2 * item + odd
-            for half in range(halves):
-                lanes = slice(half * LANES, (half + 1) * LANES)
-
-                def step_at(row):
-                    return code_step(widened(source[item, row : row + HEAD, lanes])[:1])
-
-                step = step_at(4 * reach)
-                low_step = step_at(bottom + 2 * reach)
-                high_step = step_at(top + 2 * reach)
-                for part in range(2):
-                    inner[part, frame, half, :reach] = blank
-                    at = 2 * part * reach
-                    inner[part, frame, half, reach : reach + tile] = (
-                        widened(source[item, at : at + tile, lanes]) * step
-                    )
-                    inner[part, frame, half, reach + tile :] = blank
-                    at = bottom + part * reach
-                    rims[0, part, frame, half, :reach] = (
-                        widened(source[item, at : at + reach, lanes]) * low_step
-                    )
-                    rims[0, part, frame, half, reach:] = blank
-                    at = top + part * reach
-                    rims[1, part, frame, half, :reach] = blank
-                    rims[1, part, frame, half, reach:] = (
-                        widened(source[item, at : at + reach, lanes]) * high_step
-                    )
-            return carry
-
-        lax.fori_loop(0, share, fill, 0)
+    head_at = 4 * reach
+    near_at = head_at + HEAD
+    far_at = near_at + 2 * reach + HEAD
+    lower_at = pl.multiple_of(jnp.where(place[1] == 0, far_at, near_at), HEAD)
+    upper_at = pl.multiple_of(jnp.where(place[1] == 0, near_at, far_at), HEAD)
+    for part in range(2):
+        for half in range(halves):
+            inner[part, half, :reach] = blank
+
+    def fill(frame, carry):
+        own = pl.multiple_of(reach + frame * 3 * reach, reach)
+        rim = pl.multiple_of(frame * 3 * reach, reach)
+        for half in range(halves):
+            lanes = slice(half * LANES, (half + 1) * LANES)
+
+            def step_at(row):
+                return code_step(widened(gathered[frame, pl.ds(row, HEAD), lanes])[:1])
+
+            step = step_at(head_at)
+            lower_step = step_at(lower_at + 2 * reach)
+            upper_step = step_at(upper_at + 2 * reach)
+            for part in range(2):
+                at = 2 * part * reach
+                inner[part, half, pl.ds(own, tile)] = (
+                    widened(gathered[frame, at : at + tile, lanes]) * step
+                )
+                inner[part, half, pl.ds(own + tile, reach)] = blank
+                at = lower_at + part * reach
+                rims[part, half, pl.ds(rim, reach)] = (
+                    widened(gathered[frame, pl.ds(at, reach), lanes]) * lower_step
+                )
+                rims[part, half, pl.ds(rim + reach, reach)] = blank
+                at = upper_at + part * reach
+                rims[part, half, pl.ds(rim + 2 * reach, reach)] = (
+                    widened(gathered[frame, pl.ds(at, reach), lanes]) * upper_step
+                )
+        return carry
+
+    lax.fori_loop(0, frames, fill, 0, unroll=True)
 
     def one(level, carry):
-        here = slab[0] * levels + level
+        here = place[0] * levels + level
         starts, ramps = [], []
         for frame in range(frames):
             angle = angles[frame]
-            starts.append(reach - positions[frame] - shift_of(shears[angle], here, total))
+            start = positions[frame] + shift_of(shears[angle], here, total)
+            starts.append((3 * frame + 1) * reach - start)
             ramps.append((cosines[angle * levels + level], sines[angle * levels + level]))
         for chunk, around in enumerate((below, above)):
             rim_starts, rim_ramps = [], []
@@ -303,9 +320,9 @@
                 angle = around[frames + frame]
                 start = around[frame] + shift_of(shears[angle], here, total)
                 if chunk == 0:
-                    rim_starts.append(reach - jnp.maximum(start, 0))
+                    rim_starts.append((3 * frame + 1) * reach - jnp.maximum(start, 0))
                 else:
-                    rim_starts.append(-jnp.minimum(start, 0))
+                    rim_starts.append((3 * frame + 1) * reach - jnp.minimum(start, 0))
                 rim_ramps.append((cosines[angle * levels + level], sines[angle * levels + level]))
             at = slice(chunk * reach, (chunk + 1) * reach)
             for half in range(halves):
@@ -313,16 +330,12 @@
                 sum_real = jnp.zeros((reach, LANES), jnp.float32)
                 sum_imag = jnp.zeros((reach, LANES), jnp.float32)
                 for frame in range(frames):
-                    rows = pl.ds(starts[frame] + chunk * reach, reach)
-                    rim_rows = pl.ds(rim_starts[frame], reach)
-                    for real, imag, (ramp_real, ramp_imag) in (
-                        (inner[0, frame, half, rows], inner[1, frame, half, rows], ramps[frame]),
-                        (
-                            rims[chunk, 0, frame, half, rim_rows],
-                            rims[chunk, 1, frame, half, rim_rows],
-                            rim_ramps[frame],
-                        ),
+                    for source, first, (ramp_real, ramp_imag) in (
+                        (inner, starts[frame] + chunk * reach, ramps[frame]),
+                        (rims, rim_starts[frame], rim_ramps[frame]),
                     ):
+                        real = source[0, half, pl.ds(first, reach)]
+                        imag = source[1, half, pl.ds(first, reach)]
                         sum_real = sum_real + (real * ramp_real + imag * ramp_imag)
                         sum_imag = sum_imag + (imag * ramp_real - real * ramp_imag)
                 staged[0, level, at, lanes] = sum_real
@@ -339,18 +352,18 @@
     return pl.BlockSpec(memory_space=pltpu.SMEM)
 
 
-def resident(shape):
-    return pl.BlockSpec(shape, lambda *_: (0,) * len(shape), pipeline_mode=pl.Buffered(1))
+def resident():
+    return pl.BlockSpec(memory_space=pltpu.VMEM)
 
 
 def params(mebibytes):
     return pltpu.CompilerParams(vmem_limit_bytes=mebibytes << 20)
 
 
-def passed_along(value, steps):
+def exchanged(value, shift):
     count = lax.axis_size("lat")
-    initial, last = (max(0, -steps), min(count, count - steps))
-    return lax.ppermute(value, "lat", [(source, source + steps) for source in range(initial, last)])
+    pairs = [(i, ((i + shift) ^ 1) - shift) for i in range(count)]
+    return lax.ppermute(value, "lat", [(i, j) for i, j in pairs if 0 <= j < count])
 
 
 def shards(
@@ -371,106 +384,77 @@
     halves = width // LANES
     slabs = lax.axis_size("depth")
     total = levels * slabs
-    slab = lax.axis_index("depth").astype(jnp.int32).reshape(1)
+    odd = lax.axis_index("lat").astype(jnp.int32) & 1
+    place = jnp.stack([lax.axis_index("depth").astype(jnp.int32), odd])
     coded_rows = 2 * tile + HEAD
 
     spots = jnp.concatenate([positions, angle_index]).astype(jnp.bfloat16)
     spots = jnp.pad(spots[None], ((0, HEAD - 1), (0, width - 2 * frames)))
     rim_rows = 2 * levels * reach
     last = object_field[:, :, reach:].reshape(rim_rows, width)
-    start = object_field[:, :, :reach].reshape(rim_rows, width)
-    span = width // PIECES
-    rims = []
-    for piece in range(PIECES):
-        lanes = slice(piece * span, (piece + 1) * span)
-        pair = [last[:, lanes], start[:, lanes]]
-        if piece == 0:
-            pair = [jnp.concatenate([rows, spots[:, lanes]]) for rows in pair]
-        rims.append((passed_along(pair[0], 1), passed_along(pair[1], -1)))
-    below = rims[0][0][rim_rows, : 2 * frames].astype(jnp.int32)
-    above = rims[0][1][rim_rows, : 2 * frames].astype(jnp.int32)
+    first = object_field[:, :, :reach].reshape(rim_rows, width)
+    near = jnp.concatenate([jnp.where(odd == 0, last, first), spots])
+    far = jnp.concatenate([jnp.where(odd == 0, first, last), spots])
+    near = exchanged(near, 0)
+    far = exchanged(far, 1)
+    near_spots = near[rim_rows, : 2 * frames].astype(jnp.int32)
+    far_spots = far[rim_rows, : 2 * frames].astype(jnp.int32)
+    below = jnp.where(odd == 0, far_spots, near_spots)
+    above = jnp.where(odd == 0, near_spots, far_spots)
     cosines = jnp.cos(depth_phase).reshape(-1)
     sines = jnp.sin(depth_phase).reshape(-1)
 
-    received = []
-    for piece, (low, high) in enumerate(rims):
-        block = (2, levels, tile, span)
-        partials = pl.pallas_call(
-            exit_kernel,
-            out_shape=jax.ShapeDtypeStruct((frames, coded_rows, span), jnp.int16),
-            grid=(1,),
-            in_specs=[scalars()] * 6
-            + [
-                pl.BlockSpec(
-                    block, lambda _, p=piece: (0, 0, 0, p), pipeline_mode=pl.Buffered(1)
-                ),
-                resident(low.shape),
-                resident(high.shape),
-            ],
-            out_specs=pl.BlockSpec(memory_space=pl.ANY),
-            scratch_shapes=[
-                pltpu.VMEM((2, levels, span // LANES, 2 * tile, LANES), jnp.float32),
-                pltpu.VMEM((2, 2, reach, LANES), jnp.float32),
-                pltpu.VMEM((frames, coded_rows, span), jnp.int16),
-                pltpu.SemaphoreType.DMA(()),
-            ],
-            compiler_params=params(16),
-            interpret=INTERPRET,
-            name=f"exit_waves_{piece}",
-        )(slab, positions, angle_index, shear_rate, cosines, sines, object_field, low, high)
-        received.append(lax.all_to_all(partials, "depth", 0, 0))
+    partials = pl.pallas_call(
+        exit_kernel,
+        out_shape=jax.ShapeDtypeStruct((frames, coded_rows, width), jnp.int16),
+        in_specs=[scalars()] * 6 + [resident()] * 3,
+        out_specs=pl.BlockSpec(memory_space=pl.ANY),
+        scratch_shapes=[
+            pltpu.VMEM((2, levels, halves, 2 * tile, LANES), jnp.float32),
+            pltpu.VMEM((2, 2, reach, LANES), jnp.float32),
+            pltpu.VMEM((frames, coded_rows, width), jnp.int16),
+            pltpu.SemaphoreType.DMA(()),
+        ],
+        compiler_params=params(16),
+        interpret=INTERPRET,
+        name="exit_waves",
+    )(place, positions, angle_index, shear_rate, cosines, sines, object_field, near, far)
+    received = lax.all_to_all(partials, "depth", 0, 0)
 
     table = jnp.asarray(row_table(tile))
     column_high, column_low = (jnp.asarray(t) for t in column_tables(width))
     half_rows = tile + HEAD
-    back, to_above, to_below = pl.pallas_call(
+    back, near, far = pl.pallas_call(
         lambda *refs: frame_kernel(*refs, total=total),
         out_shape=[
             jax.ShapeDtypeStruct((rows, width), jnp.int16)
             for rows in (coded_rows, half_rows, half_rows)
         ],
-        grid_spec=pltpu.PrefetchScalarGridSpec(
-            num_scalar_prefetch=2,
-            grid=(1,),
-            in_specs=[resident(part.shape) for part in received]
-            + [
-                resident(probe_field.shape),
-                pl.BlockSpec((1, tile, width), lambda i, slot, count: (slot[0], 0, 0)),
-                resident(table.shape),
-                resident(column_high.shape),
-                resident(column_low.shape),
-            ],
-            out_specs=[
-                pl.BlockSpec((rows, width), lambda *_: (0, 0))
-                for rows in (coded_rows, half_rows, half_rows)
-            ],
-        ),
+        in_specs=[scalars()] * 2 + [resident()] * 6,
+        out_specs=[resident()] * 3,
         compiler_params=params(16),
         interpret=INTERPRET,
         name="far_field",
-    )(slab, frame_count, *received, probe_field, intensity, table, column_high, column_low)
-
-    bundle = jnp.concatenate([back, passed_along(to_above, 1), passed_along(to_below, -1)])
-    lanes_of = [[d for d in range(slabs) if d % 2 == core] for core in range(2)]
-    mine = lax.all_gather(bundle, "depth", axis_index_groups=lanes_of)
-    theirs = lax.ppermute(mine, "depth", [(d, d ^ 1) for d in range(slabs)])
+    )(place, frame_count, received, probe_field, intensity, table, column_high, column_low)
+
+    bundle = jnp.concatenate([back, exchanged(near, 0), exchanged(far, 1)])
+    gathered = lax.all_gather(bundle, "depth")
 
     return pl.pallas_call(
         correction_kernel,
         out_shape=jax.ShapeDtypeStruct((2, levels, tile, width), jnp.float32),
-        grid=(1,),
-        in_specs=[scalars()] * 8 + [resident(mine.shape), resident(theirs.shape)],
+        in_specs=[scalars()] * 8 + [resident()],
         out_specs=pl.BlockSpec(memory_space=pl.ANY),
         scratch_shapes=[
-            pltpu.VMEM((2, frames, halves, 2 * tile, LANES), jnp.float32),
-            pltpu.VMEM((2, 2, frames, halves, tile, LANES), jnp.float32),
+            pltpu.VMEM((2, halves, (3 * frames + 1) * reach, LANES), jnp.float32),
+            pltpu.VMEM((2, halves, 3 * frames * reach, LANES), jnp.float32),
             pltpu.VMEM((2, levels, tile, width), jnp.float32),
             pltpu.SemaphoreType.DMA(()),
         ],
         compiler_params=params(24),
         interpret=INTERPRET,
         name="corrections",
-    )(slab, positions, angle_index, below, above, shear_rate, cosines, sines, mine, theirs)
+    )(place, positions, angle_index, below, above, shear_rate, cosines, sines, gathered)
 
 
 def solution(mesh):

time: 97.8 us -> 92.6 us (0.947)
  the two profiles are of different devices: /device:TPU:249 before, /device:TPU:385 now
where the time goes in v2:
time: 92.6 us; the launch traced here: 92.2 us
  waiting for transfers between devices  30 us (32%)
  starting transfers between devices  22.5 us (24%)
  blocking collectives  17.9 us (19%)
  Pallas kernels  17 us (18%)
  other arithmetic  2.2 us (2%)
  local copies, waits for them, and re-layouts  1.7 us (2%)
  between operations  0.96 us (1%)
    all_gather x1, blocking collectives, shards(): gathered = lax.all_gather(bundle, 'depth')  17.9 us
    ppermute x4, starting transfers between devices, exchanged(): lax.ppermute(value, 'lat', [(i, j) for i, j in pairs if 0 <= j < count])  16.2 us
    all_to_all x1, waiting for transfers between devices, shards(): received = lax.all_to_all(partials, 'depth', 0, 0)  15.2 us
    ppermute x4, waiting for transfers between devices, exchanged(): lax.ppermute(value, 'lat', [(i, j) for i, j in pairs if 0 <= j < count])  14.8 us
    pallas_call x1, Pallas kernels, shards(): pl.pallas_call(correction_kernel, out_shape=jax.ShapeDtypeStruct((2, leve...  9.57 us
    all_to_all x1, starting transfers between devices, shards(): received = lax.all_to_all(partials, 'depth', 0, 0)  6.3 us
    pallas_call x1, Pallas kernels, shards(): pl.pallas_call(exit_kernel, out_shape=jax.ShapeDtypeStruct((frames, coded...  4.66 us
    pallas_call x1, Pallas kernels, shards(): pl.pallas_call(lambda *refs: frame_kernel(*refs, total=total), out_shape=...  2.8 us
  transfers between devices with their start and end apart: 5, of which 4 were waited for; matrix products, arithmetic and copies ran while one was open for 1% of the time, Pallas kernels for 0%

profile of v2, /device:TPU:385, one launch (start us, length us, event | category | flops | bytes accessed | tf_op | source)
XLA Modules:
  0.0 92.2 jit_solution(8670607027399912919)
XLA Ops:
  0.0 0.7 convert_bitcast_fusion
  0.7 0.1 fusion.5
  0.8 1.3 %broadcast_select_fusion = (bf16[2,8,64,256]{3,2,1,0:T(8,128)(2,1)S(1)}, bf16[2,8,64,256]{3,2,1,0:T(8,128)(2,1)S(1)}) fusion(pred[]{:T(512)S(6)} %eq.2, bf16[2,8,128,256]{3,2,1,0:T(8,128)(2,1)} %own.1), kind=kLoop, calls=%fused_computation.2 | loop fusion | flops 524288 | bytes 2097153 | tf_op jit(solution)/shard_map/jit(_where)/select_n | solution.py:396
  2.0 0.0 copy-start.19
  2.0 0.0 copy-start
  2.1 0.0 copy-start.13
  2.1 0.0 copy-start.15
  2.1 0.0 copy-start.17
  2.1 0.1 pad_maximum_fusion
  2.2 3.3 %collective-permute-start.1 = (bf16[1040,256]{1,0:T(8,128)(2,1)S(1)}, bf16[1040,256]{1,0:T(8,128)(2,1)S(1)}, u32[]{:S(2)}, u32[]{:S(2)}) collective-permute-start(bf16[1040,256]{1,0:T(8,128)(2,1)S(1)} %get-tuple-element.15), channel_id=1, source_target_pairs={{0,1},{1,0},{2,3},{3,2},{4,5},{5,4},{6,7},{7,6},{8,9},{9,8},{10,11... | collective-permute-start | bytes 1597448 | tf_op jit(solution)/shard_map/ppermute | solution.py:366
  5.5 5.5 %collective-permute-start = (bf16[1040,256]{1,0:T(8,128)(2,1)S(1)}, bf16[1040,256]{1,0:T(8,128)(2,1)S(1)}, u32[]{:S(2)}, u32[]{:S(2)}) collective-permute-start(bf16[1040,256]{1,0:T(8,128)(2,1)S(1)} %get-tuple-element.16), channel_id=1, source_target_pairs={{1,2},{2,1},{3,4},{4,3},{5,6},{6,5},{7,8},{8,7},{9,10},{10,9},{11,... | collective-permute-start | bytes 1597448 | tf_op jit(solution)/shard_map/ppermute | solution.py:366
  11.0 0.1 copy.13
  11.1 0.1 reshape.50.sines
  11.2 0.1 copy.12
  11.3 0.1 reshape.49.cosines
  11.4 0.1 pad_add_fusion.1.place.refs_0_
  11.5 5.7 %collective-permute-done.1.near = bf16[1040,256]{1,0:T(8,128)(2,1)S(1)} collective-permute-done((bf16[1040,256]{1,0:T(8,128)(2,1)S(1)}, bf16[1040,256]{1,0:T(8,128)(2,1)S(1)}, u32[]{:S(2)}, u32[]{:S(2)}) %collective-permute-start.1) | collective-permute-done | bytes 532512 | tf_op jit(solution)/shard_map/ppermute | solution.py:366
  17.2 6.2 %collective-permute-done.far = bf16[1040,256]{1,0:T(8,128)(2,1)S(1)} collective-permute-done((bf16[1040,256]{1,0:T(8,128)(2,1)S(1)}, bf16[1040,256]{1,0:T(8,128)(2,1)S(1)}, u32[]{:S(2)}, u32[]{:S(2)}) %collective-permute-start) | collective-permute-done | bytes 532512 | tf_op jit(solution)/shard_map/ppermute | solution.py:366
  23.4 4.7 %exit_waves.1 = s16[8,272,256]{2,1,0:T(8,128)(2,1)} custom-call(s32[2]{0:T(128)S(1)} %pad_add_fusion.1.place.refs_0_, s32[8]{0:T(128)S(1)} %copy-done.13, s32[8]{0:T(128)S(1)} %copy-done.15, s32[32]{0:T(128)S(1)} %copy-done.17, f32[256]{0:T(256)S(1)} %reshape.49.cosines, f32[256]{0:T(256)S(1)} %reshape.50.sines, bf16[2,8,128,256]{3,2,1,0:T(8,128)(2,1)S(1)} %copy-done, ...), custom_call_target="tpu_custom_call" | custom-call | tf_op jit(solution)/shard_map/exit_waves/pallas_call | solution.py:407
  28.1 0.6 copy-done.10
  28.7 0.0 copy-start.5
  28.7 6.3 %all-to-all-start = ((s16[8,272,256]{2,1,0:T(8,128)(2,1)}), s16[8,272,256]{2,1,0:T(8,128)(2,1)S(1)}, u32[]{:S(2)}, u32[]{:S(2)}) async-start(s16[8,272,256]{2,1,0:T(8,128)(2,1)} %exit_waves.1), calls=%async_computation | async-start | bytes 2228224 | tf_op jit(solution)/shard_map/all_to_all | solution.py:422
  35.6 15.2 %all-to-all-done.refs_2_ = s16[8,272,256]{2,1,0:T(8,128)(2,1)S(1)} async-done(((s16[8,272,256]{2,1,0:T(8,128)(2,1)}), s16[8,272,256]{2,1,0:T(8,128)(2,1)S(1)}, u32[]{:S(2)}, u32[]{:S(2)}) %all-to-all-start) | async-done | bytes 1114144 | tf_op jit(solution)/shard_map/all_to_all | solution.py:422
  50.8 0.7 copy-done.11
  51.5 2.8 %far_field.1 = (s16[272,256]{1,0:T(8,128)(2,1)S(1)}, s16[144,256]{1,0:T(8,128)(2,1)S(1)}, s16[144,256]{1,0:T(8,128)(2,1)S(1)}) custom-call(s32[2]{0:T(128)S(1)} %copy-done.11, s32[1]{0:T(128)S(6)} %copy.14.refs_1_, s16[8,272,256]{2,1,0:T(8,128)(2,1)S(1)} %all-to-all-done.refs_2_, bf16[2,128,256]{2,1,0:T(8,128)(2,1)S(1)} %copy-done.5, ...), custom_call_target="tpu_custom_call" | custom-call | tf_op jit(solution)/shard_map/far_field/pallas_call | solution.py:427
  54.3 1.9 %collective-permute-start.2 = (s16[144,256]{1,0:T(8,128)(2,1)S(1)}, s16[144,256]{1,0:T(8,128)(2,1)S(1)}, u32[]{:S(2)}, u32[]{:S(2)}) collective-permute-start(s16[144,256]{1,0:T(8,128)(2,1)S(1)} %get-tuple-element.9), channel_id=1, source_target_pairs={{0,1},{1,0},{2,3},{3,2},{4,5},{5,4},{6,7},{7,6},{8,9},{9,8},{10,11... | collective-permute-start | bytes 221192 | tf_op jit(solution)/shard_map/ppermute | solution.py:366
  56.2 5.5 %collective-permute-start.3 = (s16[144,256]{1,0:T(8,128)(2,1)S(1)}, s16[144,256]{1,0:T(8,128)(2,1)S(1)}, u32[]{:S(2)}, u32[]{:S(2)}) collective-permute-start(s16[144,256]{1,0:T(8,128)(2,1)S(1)} %get-tuple-element.10), channel_id=1, source_target_pairs={{1,2},{2,1},{3,4},{4,3},{5,6},{6,5},{7,8},{8,7},{9,10},{10,9},{11,... | collective-permute-start | bytes 221192 | tf_op jit(solution)/shard_map/ppermute | solution.py:366
  61.7 2.9 %collective-permute-done.3 = s16[144,256]{1,0:T(8,128)(2,1)S(1)} collective-permute-done((s16[144,256]{1,0:T(8,128)(2,1)S(1)}, s16[144,256]{1,0:T(8,128)(2,1)S(1)}, u32[]{:S(2)}, u32[]{:S(2)}) %collective-permute-start.3) | collective-permute-done | bytes 73760 | tf_op jit(solution)/shard_map/ppermute | solution.py:366
  64.7 0.0 copy-start.16
  64.7 0.0 copy-start.18
  64.7 17.9 %all-gather.2 = s16[4480,256]{1,0:T(8,128)(2,1)S(1)} all-gather(s16[560,256]{1,0:T(8,128)(2,1)S(1)} %pad_add_fusion), channel_id=2, replica_groups=mesh['depth'=8,'lat'=64] {'depth'}, dimensions={0}, use_global_device_ids=true | all-gather | bytes 2580480 | tf_op jit(solution)/shard_map/all_gather | solution.py:441
  82.7 9.6 %corrections.1 = f32[2,8,128,256]{3,2,1,0:T(8,128)} custom-call(s32[2]{0:T(128)S(1)} %copy-done.12, s32[8]{0:T(128)S(1)} %copy-done.14, s32[8]{0:T(128)S(1)} %copy-done.16, s32[16]{0:T(128)S(1)} %get-tuple-element.12.below, s32[16]{0:T(128)S(1)} %get-tuple-element.11.above, s32[32]{0:T(128)S(1)} %copy-done.18, f32[256]{0:T(256)S(1)} %copy-done.9, ...), custom_call_target="tpu_custom_call" | custom-call | tf_op jit(solution)/shard_map/corrections/pallas_call | solution.py:443
  (34 shorter events, 0.1 us)
Async XLA Ops:
  2.0 9.0 %copy-start.19 = (f32[32,8]{0,1:T(8,128)S(1)}, f32[32,8]{0,1:T(8,128)}, u32[]{:S(2)}) copy-start(f32[32,8]{0,1:T(8,128)} %param.14) | copy-start | bytes 3076
  2.0 21.3 %copy-start = (bf16[2,8,128,256]{3,2,1,0:T(8,128)(2,1)S(1)}, bf16[2,8,128,256]{3,2,1,0:T(8,128)(2,1)}, u32[]{:S(2)}) copy-start(bf16[2,8,128,256]{3,2,1,0:T(8,128)(2,1)} %own.1) | copy-start | bytes 3145732
  2.1 21.3 %copy-start.13 = (s32[8]{0:T(128)S(1)}, s32[8]{0:T(128)}, u32[]{:S(2)}) copy-start(s32[8]{0:T(128)} %positions.3) | copy-start | bytes 100
  2.1 21.3 %copy-start.15 = (s32[8]{0:T(128)S(1)}, s32[8]{0:T(128)}, u32[]{:S(2)}) copy-start(s32[8]{0:T(128)} %angles.3) | copy-start | bytes 100
  2.1 21.3 %copy-start.17 = (s32[32]{0:T(128)S(1)}, s32[32]{0:T(128)}, u32[]{:S(2)}) copy-start(s32[32]{0:T(128)} %shears.3) | copy-start | bytes 388
  2.2 15.0 %collective-permute-start.1 = (bf16[1040,256]{1,0:T(8,128)(2,1)S(1)}, bf16[1040,256]{1,0:T(8,128)(2,1)S(1)}, u32[]{:S(2)}, u32[]{:S(2)}) collective-permute-start(bf16[1040,256]{1,0:T(8,128)(2,1)S(1)} %get-tuple-element.15), channel_id=1, source_target_pairs={{0,1},{1,0},{2,3},{3,2},{4,5},{5,4},{6,7},{7,6},{8,9},{9,8},{10,11... | collective-permute-start | bytes 1597448 | tf_op jit(solution)/shard_map/ppermute | solution.py:366
  5.5 17.9 %collective-permute-start = (bf16[1040,256]{1,0:T(8,128)(2,1)S(1)}, bf16[1040,256]{1,0:T(8,128)(2,1)S(1)}, u32[]{:S(2)}, u32[]{:S(2)}) collective-permute-start(bf16[1040,256]{1,0:T(8,128)(2,1)S(1)} %get-tuple-element.16), channel_id=1, source_target_pairs={{1,2},{2,1},{3,4},{4,3},{5,6},{6,5},{7,8},{8,7},{9,10},{10,9},{11,... | collective-permute-start | bytes 1597448 | tf_op jit(solution)/shard_map/ppermute | solution.py:366
  11.2 16.9 %copy-start.6 = (f32[256]{0:T(256)}, f32[256]{0:T(256)S(1)}, u32[]{:S(2)}) copy-start(f32[256]{0:T(256)S(1)} %reshape.50.sines) | copy-start | bytes 3076
  11.4 16.7 %copy-start.8 = (f32[256]{0:T(256)}, f32[256]{0:T(256)S(1)}, u32[]{:S(2)}) copy-start(f32[256]{0:T(256)S(1)} %reshape.49.cosines) | copy-start | bytes 3076
  28.1 0.6 copy-start.10
  28.7 22.1 %copy-start.1 = (bf16[8,128,256]{2,1,0:T(8,128)(2,1)S(1)}, bf16[8,128,256]{2,1,0:T(8,128)(2,1)}, u32[]{:S(2)}) copy-start(bf16[8,128,256]{2,1,0:T(8,128)(2,1)} %refs_4_.1) | copy-start | bytes 1572868
  28.7 22.1 %copy-start.2 = (bf16[256,512]{1,0:T(8,128)(2,1)S(1)}, bf16[256,512]{1,0:T(8,128)(2,1)}, u32[]{:S(2)}) copy-start(bf16[256,512]{1,0:T(8,128)(2,1)} %constant.23.clone.refs_7_) | copy-start | bytes 786436
  28.7 22.1 %copy-start.3 = (bf16[256,512]{1,0:T(8,128)(2,1)S(1)}, bf16[256,512]{1,0:T(8,128)(2,1)}, u32[]{:S(2)}) copy-start(bf16[256,512]{1,0:T(8,128)(2,1)} %constant.22.clone.refs_6_) | copy-start | bytes 786436
  28.7 22.1 %copy-start.4 = (bf16[256,384]{1,0:T(8,128)(2,1)S(1)}, bf16[256,384]{1,0:T(8,128)(2,1)}, u32[]{:S(2)}) copy-start(bf16[256,384]{1,0:T(8,128)(2,1)} %constant.21.clone.refs_5_) | copy-start | bytes 589828
  28.7 22.1 %copy-start.5 = (bf16[2,128,256]{2,1,0:T(8,128)(2,1)S(1)}, bf16[2,128,256]{2,1,0:T(8,128)(2,1)}, u32[]{:S(2)}) copy-start(bf16[2,128,256]{2,1,0:T(8,128)(2,1)} %refs_3_.1) | copy-start | bytes 393220
  28.7 22.1 %all-to-all-start = ((s16[8,272,256]{2,1,0:T(8,128)(2,1)}), s16[8,272,256]{2,1,0:T(8,128)(2,1)S(1)}, u32[]{:S(2)}, u32[]{:S(2)}) async-start(s16[8,272,256]{2,1,0:T(8,128)(2,1)} %exit_waves.1), calls=%async_computation | async-start | bytes 2228224 | tf_op jit(solution)/shard_map/all_to_all | solution.py:422
  50.8 0.7 copy-start.11
  54.3 7.4 %collective-permute-start.2 = (s16[144,256]{1,0:T(8,128)(2,1)S(1)}, s16[144,256]{1,0:T(8,128)(2,1)S(1)}, u32[]{:S(2)}, u32[]{:S(2)}) collective-permute-start(s16[144,256]{1,0:T(8,128)(2,1)S(1)} %get-tuple-element.9), channel_id=1, source_target_pairs={{0,1},{1,0},{2,3},{3,2},{4,5},{5,4},{6,7},{7,6},{8,9},{9,8},{10,11... | collective-permute-start | bytes 221192 | tf_op jit(solution)/shard_map/ppermute | solution.py:366
  56.2 8.4 %collective-permute-start.3 = (s16[144,256]{1,0:T(8,128)(2,1)S(1)}, s16[144,256]{1,0:T(8,128)(2,1)S(1)}, u32[]{:S(2)}, u32[]{:S(2)}) collective-permute-start(s16[144,256]{1,0:T(8,128)(2,1)S(1)} %get-tuple-element.10), channel_id=1, source_target_pairs={{1,2},{2,1},{3,4},{4,3},{5,6},{6,5},{7,8},{8,7},{9,10},{10,9},{11,... | collective-permute-start | bytes 221192 | tf_op jit(solution)/shard_map/ppermute | solution.py:366
  64.7 18.0 %copy-start.7 = (f32[256]{0:T(256)S(1)}, f32[256]{0:T(256)}, u32[]{:S(2)}) copy-start(f32[256]{0:T(256)} %copy-done.6) | copy-start | bytes 3076
  64.7 18.0 %copy-start.9 = (f32[256]{0:T(256)S(1)}, f32[256]{0:T(256)}, u32[]{:S(2)}) copy-start(f32[256]{0:T(256)} %copy-done.8) | copy-start | bytes 3076
  64.7 17.9 %copy-start.12 = (s32[2]{0:T(128)S(1)}, s32[2]{0:T(128)}, u32[]{:S(2)}) copy-start(s32[2]{0:T(128)} %copy-done.10) | copy-start | bytes 28
  64.7 17.9 %copy-start.14 = (s32[8]{0:T(128)S(1)}, s32[8]{0:T(128)}, u32[]{:S(2)}) copy-start(s32[8]{0:T(128)} %positions.3) | copy-start | bytes 100
  64.7 17.9 %copy-start.16 = (s32[8]{0:T(128)S(1)}, s32[8]{0:T(128)}, u32[]{:S(2)}) copy-start(s32[8]{0:T(128)} %angles.3) | copy-start | bytes 100
  64.7 17.9 %copy-start.18 = (s32[32]{0:T(128)S(1)}, s32[32]{0:T(128)}, u32[]{:S(2)}) copy-start(s32[32]{0:T(128)} %shears.3) | copy-start | bytes 388

commit v3 on v2

--- a/solution.py
+++ b/solution.py
@@ -52,9 +52,12 @@
     return jnp.exp(code * (math.log(2.0) / STEPS)) * (1.0 / TOP)
 
 
+def whole(value, gain):
+    return ((value * gain + SHIFTER) - SHIFTER).astype(jnp.int32)
+
+
 def coded(value, gain):
-    rounded = (value * gain + SHIFTER) - SHIFTER
-    return rounded.astype(jnp.int32).astype(jnp.int16)
+    return whole(value, gain).astype(jnp.int16)
 
 
 def widened(value):
@@ -66,16 +69,30 @@
 
 
 def exit_kernel(
-    place, positions, angles, shears, cosines, sines, own, near, far, out, extended, wave, staged, sem
+    slab,
+    side,
+    positions,
+    angles,
+    shears,
+    cosines,
+    sines,
+    own,
+    near,
+    far,
+    out,
+    extended,
+    wave,
+    staged,
+    sem,
 ):
     frames = out.shape[0]
     levels, tile = own.shape[1], own.shape[2]
     reach = tile // 2
     halves = own.shape[3] // LANES
     total = 8 * levels
-    first = place[0] * levels
-    near_at = pl.multiple_of((1 - place[1]) * (reach + tile), reach)
-    far_at = pl.multiple_of(place[1] * (reach + tile), reach)
+    first = slab[0] * levels
+    near_at = pl.multiple_of((1 - side[0]) * (reach + tile), reach)
+    far_at = pl.multiple_of(side[0] * (reach + tile), reach)
 
     def fill(level, carry):
         for part in range(2):
@@ -93,7 +110,7 @@
                 )
         return carry
 
-    lax.fori_loop(0, levels, fill, 0)
+    lax.fori_loop(0, levels, fill, 0, unroll=True)
 
     def one(frame, carry):
         angle = angles[frame]
@@ -133,7 +150,7 @@
         pltpu.make_async_copy(staged.at[frame], out.at[frame], sem).start()
         return carry
 
-    lax.fori_loop(0, frames, one, 0)
+    lax.fori_loop(0, frames, one, 0, unroll=True)
     pltpu.make_async_copy(staged, out, sem).wait()
 
 
@@ -174,7 +191,8 @@
 
 
 def frame_kernel(
-    place,
+    slab,
+    side,
     count,
     *refs,
     total,
@@ -212,8 +230,8 @@
     far_imag = cos_imag - sin_real
 
     magnitude = jnp.sqrt(far_real * far_real + far_imag * far_imag)
-    amplitude = jnp.sqrt(intensity[place[0]].astype(jnp.float32))
-    valid = jnp.where(place[0] < count[0], 1.0, 0.0).astype(jnp.float32)
+    amplitude = jnp.sqrt(intensity[slab[0]].astype(jnp.float32))
+    valid = jnp.where(slab[0] < count[0], 1.0, 0.0).astype(jnp.float32)
     factor = (amplitude / jnp.maximum(magnitude, 0.5) - 1.0) * valid
     far_real = far_real * factor
     far_imag = far_imag * factor
@@ -234,31 +252,25 @@
     )
     code = column_code(peak)
     gain = code_gain(code)
-    coded_real = coded(back_real, gain)
-    coded_imag = coded(back_imag, gain)
+    rounded_real = whole(back_real, gain)
+    rounded_imag = whole(back_imag, gain)
     head = jnp.broadcast_to(code, (HEAD, code.shape[1])).astype(jnp.int32).astype(jnp.int16)
-    out[: 2 * reach] = coded_real
-    out[2 * reach : 4 * reach] = coded_imag
+    out[: 2 * reach] = rounded_real.astype(jnp.int16)
+    out[2 * reach : 4 * reach] = rounded_imag.astype(jnp.int16)
     out[4 * reach :] = head
 
-    def rims(first_out, last_out):
-        first_out[:reach] = coded_real[:reach]
-        first_out[reach : 2 * reach] = coded_imag[:reach]
-        first_out[2 * reach :] = head
-        last_out[:reach] = coded_real[reach:]
-        last_out[reach : 2 * reach] = coded_imag[reach:]
-        last_out[2 * reach :] = head
-
-    @pl.when(place[1] == 0)
-    def _():
-        rims(far_out, near_out)
-
-    @pl.when(place[1] == 1)
-    def _():
-        rims(near_out, far_out)
-
-
-def correction_kernel(place, positions, angles, below, above, shears, cosines, sines, *refs):
+    even = side[0] == 0
+    for part, value in enumerate((rounded_real, rounded_imag)):
+        rows = slice(part * reach, (part + 1) * reach)
+        near_out[rows] = jnp.where(even, value[reach:], value[:reach]).astype(jnp.int16)
+        far_out[rows] = jnp.where(even, value[:reach], value[reach:]).astype(jnp.int16)
+    near_out[2 * reach :] = head
+    far_out[2 * reach :] = head
+
+
+def correction_kernel(
+    slab, side, positions, angles, below, above, shears, cosines, sines, *refs
+):
     gathered, out, inner, rims, staged, sem = refs
     levels, tile = out.shape[1], out.shape[2]
     reach = tile // 2
@@ -269,8 +281,8 @@
     head_at = 4 * reach
     near_at = head_at + HEAD
     far_at = near_at + 2 * reach + HEAD
-    lower_at = pl.multiple_of(jnp.where(place[1] == 0, far_at, near_at), HEAD)
-    upper_at = pl.multiple_of(jnp.where(place[1] == 0, near_at, far_at), HEAD)
+    lower_at = pl.multiple_of(jnp.where(side[0] == 0, far_at, near_at), HEAD)
+    upper_at = pl.multiple_of(jnp.where(side[0] == 0, near_at, far_at), HEAD)
     for part in range(2):
         for half in range(halves):
             inner[part, half, :reach] = blank
@@ -307,7 +319,7 @@
     lax.fori_loop(0, frames, fill, 0, unroll=True)
 
     def one(level, carry):
-        here = place[0] * levels + level
+        here = slab[0] * levels + level
         starts, ramps = [], []
         for frame in range(frames):
             angle = angles[frame]
@@ -344,7 +356,7 @@
             pltpu.make_async_copy(staged.at[part, level], out.at[part, level], sem).start()
         return carry
 
-    lax.fori_loop(0, levels, one, 0)
+    lax.fori_loop(0, levels, one, 0, unroll=True)
     pltpu.make_async_copy(staged, out, sem).wait()
 
 
@@ -385,7 +397,8 @@
     slabs = lax.axis_size("depth")
     total = levels * slabs
     odd = lax.axis_index("lat").astype(jnp.int32) & 1
-    place = jnp.stack([lax.axis_index("depth").astype(jnp.int32), odd])
+    slab = lax.axis_index("depth").astype(jnp.int32).reshape(1)
+    side = odd.reshape(1)
     coded_rows = 2 * tile + HEAD
 
     spots = jnp.concatenate([positions, angle_index]).astype(jnp.bfloat16)
@@ -407,7 +420,7 @@
     partials = pl.pallas_call(
         exit_kernel,
         out_shape=jax.ShapeDtypeStruct((frames, coded_rows, width), jnp.int16),
-        in_specs=[scalars()] * 6 + [resident()] * 3,
+        in_specs=[scalars()] * 7 + [resident()] * 3,
         out_specs=pl.BlockSpec(memory_space=pl.ANY),
         scratch_shapes=[
             pltpu.VMEM((2, levels, halves, 2 * tile, LANES), jnp.float32),
@@ -418,7 +431,7 @@
         compiler_params=params(16),
         interpret=INTERPRET,
         name="exit_waves",
-    )(place, positions, angle_index, shear_rate, cosines, sines, object_field, near, far)
+    )(slab, side, positions, angle_index, shear_rate, cosines, sines, object_field, near, far)
     received = lax.all_to_all(partials, "depth", 0, 0)
 
     table = jnp.asarray(row_table(tile))
@@ -430,12 +443,12 @@
             jax.ShapeDtypeStruct((rows, width), jnp.int16)
             for rows in (coded_rows, half_rows, half_rows)
         ],
-        in_specs=[scalars()] * 2 + [resident()] * 6,
+        in_specs=[scalars()] * 3 + [resident()] * 6,
         out_specs=[resident()] * 3,
         compiler_params=params(16),
         interpret=INTERPRET,
         name="far_field",
-    )(place, frame_count, received, probe_field, intensity, table, column_high, column_low)
+    )(slab, side, frame_count, received, probe_field, intensity, table, column_high, column_low)
 
     bundle = jnp.concatenate([back, exchanged(near, 0), exchanged(far, 1)])
     gathered = lax.all_gather(bundle, "depth")
@@ -443,7 +456,7 @@
     return pl.pallas_call(
         correction_kernel,
         out_shape=jax.ShapeDtypeStruct((2, levels, tile, width), jnp.float32),
-        in_specs=[scalars()] * 8 + [resident()],
+        in_specs=[scalars()] * 9 + [resident()],
         out_specs=pl.BlockSpec(memory_space=pl.ANY),
         scratch_shapes=[
             pltpu.VMEM((2, halves, (3 * frames + 1) * reach, LANES), jnp.float32),
@@ -454,7 +467,7 @@
         compiler_params=params(24),
         interpret=INTERPRET,
         name="corrections",
-    )(place, positions, angle_index, below, above, shear_rate, cosines, sines, gathered)
+    )(slab, side, positions, angle_index, below, above, shear_rate, cosines, sines, gathered)
 
 
 def solution(mesh):

time: 92.6 us -> 87.5 us (0.945)
  Pallas kernels: 17 us -> 13.3 us
  local copies, waits for them, and re-layouts: 1.7 us -> 0.48 us
    pallas_call x1, Pallas kernels: 9.57 us -> 6.52 us  [shards(): pl.pallas_call(correction_kernel, out_shape=jax.ShapeDtypeStruct((2, leve...]
    unnamed x40 -> x34, local copies, waits for them, and re-layouts: 1.33 us -> 0.1 us
  transfers between devices with their start and end apart: 5 -> 5, of which waited for: 4 -> 4; matrix products, arithmetic and copies ran while one was open for 1% -> 0% of each run, Pallas kernels for 0% -> 0%
where the time goes in v3:
time: 87.5 us; the launch traced here: 87.2 us
  waiting for transfers between devices  30.1 us (34%)
  starting transfers between devices  22.5 us (26%)
  blocking collectives  17.9 us (20%)
  Pallas kernels  13.3 us (15%)
  other arithmetic  2.13 us (2%)
  between operations  0.95 us (1%)
    all_gather x1, blocking collectives, shards(): gathered = lax.all_gather(bundle, 'depth')  17.9 us
    ppermute x4, starting transfers between devices, exchanged(): lax.ppermute(value, 'lat', [(i, j) for i, j in pairs if 0 <= j < count])  16.2 us
    all_to_all x1, waiting for transfers between devices, shards(): received = lax.all_to_all(partials, 'depth', 0, 0)  15.2 us
    ppermute x4, waiting for transfers between devices, exchanged(): lax.ppermute(value, 'lat', [(i, j) for i, j in pairs if 0 <= j < count])  14.9 us
    pallas_call x1, Pallas kernels, shards(): pl.pallas_call(correction_kernel, out_shape=jax.ShapeDtypeStruct((2, leve...  6.52 us
    all_to_all x1, starting transfers between devices, shards(): received = lax.all_to_all(partials, 'depth', 0, 0)  6.3 us
    pallas_call x1, Pallas kernels, shards(): pl.pallas_call(exit_kernel, out_shape=jax.ShapeDtypeStruct((frames, coded...  4.47 us
    pallas_call x1, Pallas kernels, shards(): pl.pallas_call(lambda *refs: frame_kernel(*refs, total=total), out_shape=...  2.26 us
  transfers between devices with their start and end apart: 5, of which 4 were waited for; matrix products, arithmetic and copies ran while one was open for 0% of the time, Pallas kernels for 0%

profile of v3, /device:TPU:385, one launch (start us, length us, event | category | flops | bytes accessed | tf_op | source)
XLA Modules:
  0.0 87.2 jit_solution(12957055952685412032)
XLA Ops:
  0.0 0.7 convert_bitcast_fusion
  0.7 0.1 fusion.5
  0.8 1.3 %broadcast_select_fusion = (bf16[2,8,64,256]{3,2,1,0:T(8,128)(2,1)S(1)}, bf16[2,8,64,256]{3,2,1,0:T(8,128)(2,1)S(1)}) fusion(pred[]{:T(512)S(6)} %eq.2, bf16[2,8,128,256]{3,2,1,0:T(8,128)(2,1)} %own.1), kind=kLoop, calls=%fused_computation.2 | loop fusion | flops 524288 | bytes 2097153 | tf_op jit(solution)/shard_map/jit(_where)/select_n | solution.py:409
  2.0 0.0 copy-start.16
  2.0 0.0 copy-start
  2.1 0.0 copy-start.10
  2.1 0.0 copy-start.12
  2.1 0.1 pad_maximum_fusion
  2.2 3.3 %collective-permute-start.1 = (bf16[1040,256]{1,0:T(8,128)(2,1)S(1)}, bf16[1040,256]{1,0:T(8,128)(2,1)S(1)}, u32[]{:S(2)}, u32[]{:S(2)}) collective-permute-start(bf16[1040,256]{1,0:T(8,128)(2,1)S(1)} %get-tuple-element.15), channel_id=1, source_target_pairs={{0,1},{1,0},{2,3},{3,2},{4,5},{5,4},{6,7},{7,6},{8,9},{9,8},{10,11... | collective-permute-start | bytes 1597448 | tf_op jit(solution)/shard_map/ppermute | solution.py:378
  5.5 5.5 %collective-permute-start = (bf16[1040,256]{1,0:T(8,128)(2,1)S(1)}, bf16[1040,256]{1,0:T(8,128)(2,1)S(1)}, u32[]{:S(2)}, u32[]{:S(2)}) collective-permute-start(bf16[1040,256]{1,0:T(8,128)(2,1)S(1)} %get-tuple-element.16), channel_id=1, source_target_pairs={{1,2},{2,1},{3,4},{4,3},{5,6},{6,5},{7,8},{8,7},{9,10},{10,9},{11,... | collective-permute-start | bytes 1597448 | tf_op jit(solution)/shard_map/ppermute | solution.py:378
  11.0 0.1 copy.13
  11.1 0.1 reshape.58.sines
  11.2 0.1 copy.12
  11.3 0.1 reshape.57.cosines
  11.4 5.8 %collective-permute-done.1.near = bf16[1040,256]{1,0:T(8,128)(2,1)S(1)} collective-permute-done((bf16[1040,256]{1,0:T(8,128)(2,1)S(1)}, bf16[1040,256]{1,0:T(8,128)(2,1)S(1)}, u32[]{:S(2)}, u32[]{:S(2)}) %collective-permute-start.1) | collective-permute-done | bytes 532512 | tf_op jit(solution)/shard_map/ppermute | solution.py:378
  17.2 6.2 %collective-permute-done.far = bf16[1040,256]{1,0:T(8,128)(2,1)S(1)} collective-permute-done((bf16[1040,256]{1,0:T(8,128)(2,1)S(1)}, bf16[1040,256]{1,0:T(8,128)(2,1)S(1)}, u32[]{:S(2)}, u32[]{:S(2)}) %collective-permute-start) | collective-permute-done | bytes 532512 | tf_op jit(solution)/shard_map/ppermute | solution.py:378
  23.4 4.5 %exit_waves.1 = s16[8,272,256]{2,1,0:T(8,128)(2,1)} custom-call(s32[1]{0:T(128)} %bitcast.slab.refs_0_, s32[1]{0:T(128)} %bitcast.1.side.refs_1_, s32[8]{0:T(128)S(1)} %copy-done.10, s32[8]{0:T(128)S(1)} %copy-done.12, s32[32]{0:T(128)S(1)} %copy-done.14, f32[256]{0:T(256)S(1)} %reshape.57.cosines, f32[256]{0:T(256)S(1)} %reshape.58.sines, ...), custom_call_target="tpu_custom_call" | custom-call | tf_op jit(solution)/shard_map/exit_waves/pallas_call | solution.py:420
  27.9 0.0 copy-start.1
  27.9 0.0 copy-start.2
  27.9 0.0 copy-start.3
  27.9 0.0 copy-start.4
  27.9 0.0 copy-start.5
  28.0 6.3 %all-to-all-start = ((s16[8,272,256]{2,1,0:T(8,128)(2,1)}), s16[8,272,256]{2,1,0:T(8,128)(2,1)S(1)}, u32[]{:S(2)}, u32[]{:S(2)}) async-start(s16[8,272,256]{2,1,0:T(8,128)(2,1)} %exit_waves.1), calls=%async_computation | async-start | bytes 2228224 | tf_op jit(solution)/shard_map/all_to_all | solution.py:435
  34.9 15.2 %all-to-all-done.refs_3_ = s16[8,272,256]{2,1,0:T(8,128)(2,1)S(1)} async-done(((s16[8,272,256]{2,1,0:T(8,128)(2,1)}), s16[8,272,256]{2,1,0:T(8,128)(2,1)S(1)}, u32[]{:S(2)}, u32[]{:S(2)}) %all-to-all-start) | async-done | bytes 1114144 | tf_op jit(solution)/shard_map/all_to_all | solution.py:435
  50.1 2.3 %far_field.1 = (s16[272,256]{1,0:T(8,128)(2,1)S(1)}, s16[144,256]{1,0:T(8,128)(2,1)S(1)}, s16[144,256]{1,0:T(8,128)(2,1)S(1)}) custom-call(s32[1]{0:T(128)} %bitcast.slab.refs_0_, s32[1]{0:T(128)} %bitcast.1.side.refs_1_, s32[1]{0:T(128)S(6)} %copy.14.refs_2_, s16[8,272,256]{2,1,0:T(8,128)(2,1)S(1)} %all-to-all-done.refs_3_, ...), custom_call_target="tpu_custom_call" | custom-call | tf_op jit(solution)/shard_map/far_field/pallas_call | solution.py:440
  52.4 1.9 %collective-permute-start.2 = (s16[144,256]{1,0:T(8,128)(2,1)S(1)}, s16[144,256]{1,0:T(8,128)(2,1)S(1)}, u32[]{:S(2)}, u32[]{:S(2)}) collective-permute-start(s16[144,256]{1,0:T(8,128)(2,1)S(1)} %get-tuple-element.9), channel_id=1, source_target_pairs={{0,1},{1,0},{2,3},{3,2},{4,5},{5,4},{6,7},{7,6},{8,9},{9,8},{10,11... | collective-permute-start | bytes 221192 | tf_op jit(solution)/shard_map/ppermute | solution.py:378
  54.3 5.4 %collective-permute-start.3 = (s16[144,256]{1,0:T(8,128)(2,1)S(1)}, s16[144,256]{1,0:T(8,128)(2,1)S(1)}, u32[]{:S(2)}, u32[]{:S(2)}) collective-permute-start(s16[144,256]{1,0:T(8,128)(2,1)S(1)} %get-tuple-element.10), channel_id=1, source_target_pairs={{1,2},{2,1},{3,4},{4,3},{5,6},{6,5},{7,8},{8,7},{9,10},{10,9},{11,... | collective-permute-start | bytes 221192 | tf_op jit(solution)/shard_map/ppermute | solution.py:378
  59.8 2.9 %collective-permute-done.3 = s16[144,256]{1,0:T(8,128)(2,1)S(1)} collective-permute-done((s16[144,256]{1,0:T(8,128)(2,1)S(1)}, s16[144,256]{1,0:T(8,128)(2,1)S(1)}, u32[]{:S(2)}, u32[]{:S(2)}) %collective-permute-start.3) | collective-permute-done | bytes 73760 | tf_op jit(solution)/shard_map/ppermute | solution.py:378
  62.8 0.0 copy-start.13
  62.8 0.0 copy-start.15
  62.8 17.9 %all-gather.2 = s16[4480,256]{1,0:T(8,128)(2,1)S(1)} all-gather(s16[560,256]{1,0:T(8,128)(2,1)S(1)} %pad_add_fusion), channel_id=2, replica_groups=mesh['depth'=8,'lat'=64] {'depth'}, dimensions={0}, use_global_device_ids=true | all-gather | bytes 2580480 | tf_op jit(solution)/shard_map/all_gather | solution.py:454
  80.7 6.5 %corrections.1 = f32[2,8,128,256]{3,2,1,0:T(8,128)} custom-call(s32[1]{0:T(128)} %bitcast.slab.refs_0_, s32[1]{0:T(128)} %bitcast.1.side.refs_1_, s32[8]{0:T(128)S(1)} %copy-done.11, s32[8]{0:T(128)S(1)} %copy-done.13, s32[16]{0:T(128)S(1)} %get-tuple-element.12.below, s32[16]{0:T(128)S(1)} %get-tuple-element.11.above, s32[32]{0:T(128)S(1)} %copy-done.15, ...), custom_call_target="tpu_custom_call" | custom-call | tf_op jit(solution)/shard_map/corrections/pallas_call | solution.py:456
  (27 shorter events, 0.1 us)
Async XLA Ops:
  2.0 9.0 %copy-start.16 = (f32[32,8]{0,1:T(8,128)S(1)}, f32[32,8]{0,1:T(8,128)}, u32[]{:S(2)}) copy-start(f32[32,8]{0,1:T(8,128)} %param.14) | copy-start | bytes 3076
  2.0 21.3 %copy-start = (bf16[2,8,128,256]{3,2,1,0:T(8,128)(2,1)S(1)}, bf16[2,8,128,256]{3,2,1,0:T(8,128)(2,1)}, u32[]{:S(2)}) copy-start(bf16[2,8,128,256]{3,2,1,0:T(8,128)(2,1)} %own.1) | copy-start | bytes 3145732
  2.1 21.3 %copy-start.10 = (s32[8]{0:T(128)S(1)}, s32[8]{0:T(128)}, u32[]{:S(2)}) copy-start(s32[8]{0:T(128)} %positions.3) | copy-start | bytes 100
  2.1 21.3 %copy-start.12 = (s32[8]{0:T(128)S(1)}, s32[8]{0:T(128)}, u32[]{:S(2)}) copy-start(s32[8]{0:T(128)} %angles.3) | copy-start | bytes 100
  2.1 21.3 %copy-start.14 = (s32[32]{0:T(128)S(1)}, s32[32]{0:T(128)}, u32[]{:S(2)}) copy-start(s32[32]{0:T(128)} %shears.3) | copy-start | bytes 388
  2.2 15.0 %collective-permute-start.1 = (bf16[1040,256]{1,0:T(8,128)(2,1)S(1)}, bf16[1040,256]{1,0:T(8,128)(2,1)S(1)}, u32[]{:S(2)}, u32[]{:S(2)}) collective-permute-start(bf16[1040,256]{1,0:T(8,128)(2,1)S(1)} %get-tuple-element.15), channel_id=1, source_target_pairs={{0,1},{1,0},{2,3},{3,2},{4,5},{5,4},{6,7},{7,6},{8,9},{9,8},{10,11... | collective-permute-start | bytes 1597448 | tf_op jit(solution)/shard_map/ppermute | solution.py:378
  5.5 17.9 %collective-permute-start = (bf16[1040,256]{1,0:T(8,128)(2,1)S(1)}, bf16[1040,256]{1,0:T(8,128)(2,1)S(1)}, u32[]{:S(2)}, u32[]{:S(2)}) collective-permute-start(bf16[1040,256]{1,0:T(8,128)(2,1)S(1)} %get-tuple-element.16), channel_id=1, source_target_pairs={{1,2},{2,1},{3,4},{4,3},{5,6},{6,5},{7,8},{8,7},{9,10},{10,9},{11,... | collective-permute-start | bytes 1597448 | tf_op jit(solution)/shard_map/ppermute | solution.py:378
  11.2 16.7 %copy-start.6 = (f32[256]{0:T(256)}, f32[256]{0:T(256)S(1)}, u32[]{:S(2)}) copy-start(f32[256]{0:T(256)S(1)} %reshape.58.sines) | copy-start | bytes 3076
  11.4 16.5 %copy-start.8 = (f32[256]{0:T(256)}, f32[256]{0:T(256)S(1)}, u32[]{:S(2)}) copy-start(f32[256]{0:T(256)S(1)} %reshape.57.cosines) | copy-start | bytes 3076
  27.9 22.2 %copy-start.1 = (bf16[8,128,256]{2,1,0:T(8,128)(2,1)S(1)}, bf16[8,128,256]{2,1,0:T(8,128)(2,1)}, u32[]{:S(2)}) copy-start(bf16[8,128,256]{2,1,0:T(8,128)(2,1)} %refs_5_.1) | copy-start | bytes 1572868
  27.9 22.2 %copy-start.2 = (bf16[256,512]{1,0:T(8,128)(2,1)S(1)}, bf16[256,512]{1,0:T(8,128)(2,1)}, u32[]{:S(2)}) copy-start(bf16[256,512]{1,0:T(8,128)(2,1)} %constant.23.clone.refs_8_) | copy-start | bytes 786436
  27.9 22.2 %copy-start.3 = (bf16[256,512]{1,0:T(8,128)(2,1)S(1)}, bf16[256,512]{1,0:T(8,128)(2,1)}, u32[]{:S(2)}) copy-start(bf16[256,512]{1,0:T(8,128)(2,1)} %constant.22.clone.refs_7_) | copy-start | bytes 786436
  27.9 22.1 %copy-start.4 = (bf16[256,384]{1,0:T(8,128)(2,1)S(1)}, bf16[256,384]{1,0:T(8,128)(2,1)}, u32[]{:S(2)}) copy-start(bf16[256,384]{1,0:T(8,128)(2,1)} %constant.21.clone.refs_6_) | copy-start | bytes 589828
  27.9 22.1 %copy-start.5 = (bf16[2,128,256]{2,1,0:T(8,128)(2,1)S(1)}, bf16[2,128,256]{2,1,0:T(8,128)(2,1)}, u32[]{:S(2)}) copy-start(bf16[2,128,256]{2,1,0:T(8,128)(2,1)} %refs_4_.1) | copy-start | bytes 393220
  28.0 22.1 %all-to-all-start = ((s16[8,272,256]{2,1,0:T(8,128)(2,1)}), s16[8,272,256]{2,1,0:T(8,128)(2,1)S(1)}, u32[]{:S(2)}, u32[]{:S(2)}) async-start(s16[8,272,256]{2,1,0:T(8,128)(2,1)} %exit_waves.1), calls=%async_computation | async-start | bytes 2228224 | tf_op jit(solution)/shard_map/all_to_all | solution.py:435
  52.4 7.4 %collective-permute-start.2 = (s16[144,256]{1,0:T(8,128)(2,1)S(1)}, s16[144,256]{1,0:T(8,128)(2,1)S(1)}, u32[]{:S(2)}, u32[]{:S(2)}) collective-permute-start(s16[144,256]{1,0:T(8,128)(2,1)S(1)} %get-tuple-element.9), channel_id=1, source_target_pairs={{0,1},{1,0},{2,3},{3,2},{4,5},{5,4},{6,7},{7,6},{8,9},{9,8},{10,11... | collective-permute-start | bytes 221192 | tf_op jit(solution)/shard_map/ppermute | solution.py:378
  54.3 8.4 %collective-permute-start.3 = (s16[144,256]{1,0:T(8,128)(2,1)S(1)}, s16[144,256]{1,0:T(8,128)(2,1)S(1)}, u32[]{:S(2)}, u32[]{:S(2)}) collective-permute-start(s16[144,256]{1,0:T(8,128)(2,1)S(1)} %get-tuple-element.10), channel_id=1, source_target_pairs={{1,2},{2,1},{3,4},{4,3},{5,6},{6,5},{7,8},{8,7},{9,10},{10,9},{11,... | collective-permute-start | bytes 221192 | tf_op jit(solution)/shard_map/ppermute | solution.py:378
  62.7 17.9 %copy-start.7 = (f32[256]{0:T(256)S(1)}, f32[256]{0:T(256)}, u32[]{:S(2)}) copy-start(f32[256]{0:T(256)} %copy-done.6) | copy-start | bytes 3076
  62.7 17.9 %copy-start.9 = (f32[256]{0:T(256)S(1)}, f32[256]{0:T(256)}, u32[]{:S(2)}) copy-start(f32[256]{0:T(256)} %copy-done.8) | copy-start | bytes 3076
  62.8 17.9 %copy-start.11 = (s32[8]{0:T(128)S(1)}, s32[8]{0:T(128)}, u32[]{:S(2)}) copy-start(s32[8]{0:T(128)} %positions.3) | copy-start | bytes 100
  62.8 17.9 %copy-start.13 = (s32[8]{0:T(128)S(1)}, s32[8]{0:T(128)}, u32[]{:S(2)}) copy-start(s32[8]{0:T(128)} %angles.3) | copy-start | bytes 100
  62.8 17.9 %copy-start.15 = (s32[32]{0:T(128)S(1)}, s32[32]{0:T(128)}, u32[]{:S(2)}) copy-start(s32[32]{0:T(128)} %shears.3) | copy-start | bytes 388

commit v4 on v3

--- a/solution.py
+++ b/solution.py
@@ -11,7 +11,7 @@
 
 INTERPRET = False
 LANES = 128
-HEAD = 16
+HEAD = 8
 STEPS = 128.0
 TOP = 32700.0
 SHIFTER = 12582912.0

time: 87.5 us -> 86.8 us (level)
  the two profiles are of different devices: /device:TPU:385 before, /device:TPU:257 now
where the time goes in v4:
time: 86.8 us; the launch traced here: 86.5 us
  waiting for transfers between devices  33.8 us (39%)
  starting transfers between devices  18.3 us (21%)
  blocking collectives  17.7 us (20%)
  Pallas kernels  13.2 us (15%)
  other arithmetic  2.13 us (2%)
    ppermute x4, waiting for transfers between devices, exchanged(): lax.ppermute(value, 'lat', [(i, j) for i, j in pairs if 0 <= j < count])  19 us
    all_gather x1, blocking collectives, shards(): gathered = lax.all_gather(bundle, 'depth')  17.7 us
    all_to_all x1, waiting for transfers between devices, shards(): received = lax.all_to_all(partials, 'depth', 0, 0)  14.8 us
    ppermute x4, starting transfers between devices, exchanged(): lax.ppermute(value, 'lat', [(i, j) for i, j in pairs if 0 <= j < count])  12 us
    pallas_call x1, Pallas kernels, shards(): pl.pallas_call(correction_kernel, out_shape=jax.ShapeDtypeStruct((2, leve...  6.53 us
    all_to_all x1, starting transfers between devices, shards(): received = lax.all_to_all(partials, 'depth', 0, 0)  6.29 us
    pallas_call x1, Pallas kernels, shards(): pl.pallas_call(exit_kernel, out_shape=jax.ShapeDtypeStruct((frames, coded...  4.44 us
    pallas_call x1, Pallas kernels, shards(): pl.pallas_call(lambda *refs: frame_kernel(*refs, total=total), out_shape=...  2.26 us
  transfers between devices with their start and end apart: 5, of which 4 were waited for; matrix products, arithmetic and copies ran while one was open for 0% of the time, Pallas kernels for 0%

profile of v4, /device:TPU:257, one launch (start us, length us, event | category | flops | bytes accessed | tf_op | source)
XLA Modules:
  0.0 86.5 jit_solution(16133263290057764062)
XLA Ops:
  0.0 0.7 convert_bitcast_fusion
  0.7 0.1 fusion.5
  0.8 1.3 %broadcast_select_fusion = (bf16[2,8,64,256]{3,2,1,0:T(8,128)(2,1)S(1)}, bf16[2,8,64,256]{3,2,1,0:T(8,128)(2,1)S(1)}) fusion(pred[]{:T(512)S(6)} %eq.2, bf16[2,8,128,256]{3,2,1,0:T(8,128)(2,1)} %own.1), kind=kLoop, calls=%fused_computation.2 | loop fusion | flops 524288 | bytes 2097153 | tf_op jit(solution)/shard_map/jit(_where)/select_n | solution.py:409
  2.0 0.0 copy-start.9
  2.0 0.0 copy-start
  2.1 0.0 copy-start.6
  2.1 0.0 copy-start.7
  2.1 0.0 copy-start.8
  2.1 0.1 pad_maximum_fusion
  2.2 3.3 %collective-permute-start.1 = (bf16[1032,256]{1,0:T(8,128)(2,1)S(1)}, bf16[1032,256]{1,0:T(8,128)(2,1)S(1)}, u32[]{:S(2)}, u32[]{:S(2)}) collective-permute-start(bf16[1032,256]{1,0:T(8,128)(2,1)S(1)} %get-tuple-element.17), channel_id=1, source_target_pairs={{0,1},{1,0},{2,3},{3,2},{4,5},{5,4},{6,7},{7,6},{8,9},{9,8},{10,11... | collective-permute-start | bytes 1585160 | tf_op jit(solution)/shard_map/ppermute | solution.py:378
  5.5 3.4 %collective-permute-start = (bf16[1032,256]{1,0:T(8,128)(2,1)S(1)}, bf16[1032,256]{1,0:T(8,128)(2,1)S(1)}, u32[]{:S(2)}, u32[]{:S(2)}) collective-permute-start(bf16[1032,256]{1,0:T(8,128)(2,1)S(1)} %get-tuple-element.18), channel_id=1, source_target_pairs={{1,2},{2,1},{3,4},{4,3},{5,6},{6,5},{7,8},{8,7},{9,10},{10,9},{11,... | collective-permute-start | bytes 1585160 | tf_op jit(solution)/shard_map/ppermute | solution.py:378
  8.9 0.1 copy.13
  9.0 0.1 reshape.58.sines
  9.1 0.1 copy.12
  9.2 0.1 reshape.57.cosines
  9.3 7.8 %collective-permute-done.1.near = bf16[1032,256]{1,0:T(8,128)(2,1)S(1)} collective-permute-done((bf16[1032,256]{1,0:T(8,128)(2,1)S(1)}, bf16[1032,256]{1,0:T(8,128)(2,1)S(1)}, u32[]{:S(2)}, u32[]{:S(2)}) %collective-permute-start.1) | collective-permute-done | bytes 528416 | tf_op jit(solution)/shard_map/ppermute | solution.py:378
  17.1 6.2 %collective-permute-done.far = bf16[1032,256]{1,0:T(8,128)(2,1)S(1)} collective-permute-done((bf16[1032,256]{1,0:T(8,128)(2,1)S(1)}, bf16[1032,256]{1,0:T(8,128)(2,1)S(1)}, u32[]{:S(2)}, u32[]{:S(2)}) %collective-permute-start) | collective-permute-done | bytes 528416 | tf_op jit(solution)/shard_map/ppermute | solution.py:378
  23.3 4.4 %exit_waves.1 = s16[8,264,256]{2,1,0:T(8,128)(2,1)} custom-call(s32[1]{0:T(128)} %bitcast.slab.refs_0_, s32[1]{0:T(128)} %bitcast.1.side.refs_1_, s32[8]{0:T(128)S(1)} %copy-done.6, s32[8]{0:T(128)S(1)} %copy-done.7, s32[32]{0:T(128)S(1)} %copy-done.8, f32[256]{0:T(256)S(1)} %reshape.57.cosines, f32[256]{0:T(256)S(1)} %reshape.58.sines, ...), custom_call_target="tpu_custom_call" | custom-call | tf_op jit(solution)/shard_map/exit_waves/pallas_call | solution.py:420
  27.8 0.0 copy-start.1
  27.8 0.0 copy-start.2
  27.8 0.0 copy-start.3
  27.8 0.0 copy-start.4
  27.8 0.0 copy-start.5
  27.8 6.3 %all-to-all-start = ((s16[8,264,256]{2,1,0:T(8,128)(2,1)}), s16[8,264,256]{2,1,0:T(8,128)(2,1)S(1)}, u32[]{:S(2)}, u32[]{:S(2)}) async-start(s16[8,264,256]{2,1,0:T(8,128)(2,1)} %exit_waves.1), calls=%async_computation | async-start | bytes 2162688 | tf_op jit(solution)/shard_map/all_to_all | solution.py:435
  34.8 14.8 %all-to-all-done.refs_3_ = s16[8,264,256]{2,1,0:T(8,128)(2,1)S(1)} async-done(((s16[8,264,256]{2,1,0:T(8,128)(2,1)}), s16[8,264,256]{2,1,0:T(8,128)(2,1)S(1)}, u32[]{:S(2)}, u32[]{:S(2)}) %all-to-all-start) | async-done | bytes 1081376 | tf_op jit(solution)/shard_map/all_to_all | solution.py:435
  49.6 2.3 %far_field.1 = (s16[264,256]{1,0:T(8,128)(2,1)S(1)}, s16[136,256]{1,0:T(8,128)(2,1)S(1)}, s16[136,256]{1,0:T(8,128)(2,1)S(1)}) custom-call(s32[1]{0:T(128)} %bitcast.slab.refs_0_, s32[1]{0:T(128)} %bitcast.1.side.refs_1_, s32[1]{0:T(128)S(6)} %copy.14.refs_2_, s16[8,264,256]{2,1,0:T(8,128)(2,1)S(1)} %all-to-all-done.refs_3_, ...), custom_call_target="tpu_custom_call" | custom-call | tf_op jit(solution)/shard_map/far_field/pallas_call | solution.py:440
  51.9 1.9 %collective-permute-start.2 = (s16[136,256]{1,0:T(8,128)(2,1)S(1)}, s16[136,256]{1,0:T(8,128)(2,1)S(1)}, u32[]{:S(2)}, u32[]{:S(2)}) collective-permute-start(s16[136,256]{1,0:T(8,128)(2,1)S(1)} %get-tuple-element.9), channel_id=1, source_target_pairs={{0,1},{1,0},{2,3},{3,2},{4,5},{5,4},{6,7},{7,6},{8,9},{9,8},{10,11... | collective-permute-start | bytes 208904 | tf_op jit(solution)/shard_map/ppermute | solution.py:378
  53.8 3.3 %collective-permute-start.3 = (s16[136,256]{1,0:T(8,128)(2,1)S(1)}, s16[136,256]{1,0:T(8,128)(2,1)S(1)}, u32[]{:S(2)}, u32[]{:S(2)}) collective-permute-start(s16[136,256]{1,0:T(8,128)(2,1)S(1)} %get-tuple-element.10), channel_id=1, source_target_pairs={{1,2},{2,1},{3,4},{4,3},{5,6},{6,5},{7,8},{8,7},{9,10},{10,9},{11,... | collective-permute-start | bytes 208904 | tf_op jit(solution)/shard_map/ppermute | solution.py:378
  57.2 0.0 collective-permute-done.2
  57.2 5.0 %collective-permute-done.3 = s16[136,256]{1,0:T(8,128)(2,1)S(1)} collective-permute-done((s16[136,256]{1,0:T(8,128)(2,1)S(1)}, s16[136,256]{1,0:T(8,128)(2,1)S(1)}, u32[]{:S(2)}, u32[]{:S(2)}) %collective-permute-start.3) | collective-permute-done | bytes 69664 | tf_op jit(solution)/shard_map/ppermute | solution.py:378
  62.2 17.7 %all-gather.2 = s16[4288,256]{1,0:T(8,128)(2,1)S(1)} all-gather(s16[536,256]{1,0:T(8,128)(2,1)S(1)} %pad_add_fusion), channel_id=2, replica_groups=mesh['depth'=8,'lat'=64] {'depth'}, dimensions={0}, use_global_device_ids=true | all-gather | bytes 2469888 | tf_op jit(solution)/shard_map/all_gather | solution.py:454
  79.9 6.5 %corrections.1 = f32[2,8,128,256]{3,2,1,0:T(8,128)} custom-call(s32[1]{0:T(128)} %bitcast.slab.refs_0_, s32[1]{0:T(128)} %bitcast.1.side.refs_1_, s32[8]{0:T(128)S(1)} %copy-done.6, s32[8]{0:T(128)S(1)} %copy-done.7, s32[16]{0:T(128)S(1)} %get-tuple-element.12.below, s32[16]{0:T(128)S(1)} %get-tuple-element.11.above, s32[32]{0:T(128)S(1)} %copy-done.8, ...), custom_call_target="tpu_custom_call" | custom-call | tf_op jit(solution)/shard_map/corrections/pallas_call | solution.py:456
  (13 shorter events, 0.1 us)
Async XLA Ops:
  2.0 6.9 %copy-start.9 = (f32[32,8]{0,1:T(8,128)S(1)}, f32[32,8]{0,1:T(8,128)}, u32[]{:S(2)}) copy-start(f32[32,8]{0,1:T(8,128)} %param.14) | copy-start | bytes 3076
  2.0 21.2 %copy-start = (bf16[2,8,128,256]{3,2,1,0:T(8,128)(2,1)S(1)}, bf16[2,8,128,256]{3,2,1,0:T(8,128)(2,1)}, u32[]{:S(2)}) copy-start(bf16[2,8,128,256]{3,2,1,0:T(8,128)(2,1)} %own.1) | copy-start | bytes 3145732
  2.1 21.2 %copy-start.6 = (s32[8]{0:T(128)S(1)}, s32[8]{0:T(128)}, u32[]{:S(2)}) copy-start(s32[8]{0:T(128)} %positions.3) | copy-start | bytes 100
  2.1 21.2 %copy-start.7 = (s32[8]{0:T(128)S(1)}, s32[8]{0:T(128)}, u32[]{:S(2)}) copy-start(s32[8]{0:T(128)} %angles.3) | copy-start | bytes 100
  2.1 21.2 %copy-start.8 = (s32[32]{0:T(128)S(1)}, s32[32]{0:T(128)}, u32[]{:S(2)}) copy-start(s32[32]{0:T(128)} %shears.3) | copy-start | bytes 388
  2.2 14.9 %collective-permute-start.1 = (bf16[1032,256]{1,0:T(8,128)(2,1)S(1)}, bf16[1032,256]{1,0:T(8,128)(2,1)S(1)}, u32[]{:S(2)}, u32[]{:S(2)}) collective-permute-start(bf16[1032,256]{1,0:T(8,128)(2,1)S(1)} %get-tuple-element.17), channel_id=1, source_target_pairs={{0,1},{1,0},{2,3},{3,2},{4,5},{5,4},{6,7},{7,6},{8,9},{9,8},{10,11... | collective-permute-start | bytes 1585160 | tf_op jit(solution)/shard_map/ppermute | solution.py:378
  5.5 17.8 %collective-permute-start = (bf16[1032,256]{1,0:T(8,128)(2,1)S(1)}, bf16[1032,256]{1,0:T(8,128)(2,1)S(1)}, u32[]{:S(2)}, u32[]{:S(2)}) collective-permute-start(bf16[1032,256]{1,0:T(8,128)(2,1)S(1)} %get-tuple-element.18), channel_id=1, source_target_pairs={{1,2},{2,1},{3,4},{4,3},{5,6},{6,5},{7,8},{8,7},{9,10},{10,9},{11,... | collective-permute-start | bytes 1585160 | tf_op jit(solution)/shard_map/ppermute | solution.py:378
  27.8 21.8 %copy-start.1 = (bf16[8,128,256]{2,1,0:T(8,128)(2,1)S(1)}, bf16[8,128,256]{2,1,0:T(8,128)(2,1)}, u32[]{:S(2)}) copy-start(bf16[8,128,256]{2,1,0:T(8,128)(2,1)} %refs_5_.1) | copy-start | bytes 1572868
  27.8 21.8 %copy-start.2 = (bf16[256,512]{1,0:T(8,128)(2,1)S(1)}, bf16[256,512]{1,0:T(8,128)(2,1)}, u32[]{:S(2)}) copy-start(bf16[256,512]{1,0:T(8,128)(2,1)} %constant.23.clone.refs_8_) | copy-start | bytes 786436
  27.8 21.8 %copy-start.3 = (bf16[256,512]{1,0:T(8,128)(2,1)S(1)}, bf16[256,512]{1,0:T(8,128)(2,1)}, u32[]{:S(2)}) copy-start(bf16[256,512]{1,0:T(8,128)(2,1)} %constant.22.clone.refs_7_) | copy-start | bytes 786436
  27.8 21.8 %copy-start.4 = (bf16[256,384]{1,0:T(8,128)(2,1)S(1)}, bf16[256,384]{1,0:T(8,128)(2,1)}, u32[]{:S(2)}) copy-start(bf16[256,384]{1,0:T(8,128)(2,1)} %constant.21.clone.refs_6_) | copy-start | bytes 589828
  27.8 21.8 %copy-start.5 = (bf16[2,128,256]{2,1,0:T(8,128)(2,1)S(1)}, bf16[2,128,256]{2,1,0:T(8,128)(2,1)}, u32[]{:S(2)}) copy-start(bf16[2,128,256]{2,1,0:T(8,128)(2,1)} %refs_4_.1) | copy-start | bytes 393220
  27.8 21.7 %all-to-all-start = ((s16[8,264,256]{2,1,0:T(8,128)(2,1)}), s16[8,264,256]{2,1,0:T(8,128)(2,1)S(1)}, u32[]{:S(2)}, u32[]{:S(2)}) async-start(s16[8,264,256]{2,1,0:T(8,128)(2,1)} %exit_waves.1), calls=%async_computation | async-start | bytes 2162688 | tf_op jit(solution)/shard_map/all_to_all | solution.py:435
  51.9 5.3 %collective-permute-start.2 = (s16[136,256]{1,0:T(8,128)(2,1)S(1)}, s16[136,256]{1,0:T(8,128)(2,1)S(1)}, u32[]{:S(2)}, u32[]{:S(2)}) collective-permute-start(s16[136,256]{1,0:T(8,128)(2,1)S(1)} %get-tuple-element.9), channel_id=1, source_target_pairs={{0,1},{1,0},{2,3},{3,2},{4,5},{5,4},{6,7},{7,6},{8,9},{9,8},{10,11... | collective-permute-start | bytes 208904 | tf_op jit(solution)/shard_map/ppermute | solution.py:378
  53.8 8.4 %collective-permute-start.3 = (s16[136,256]{1,0:T(8,128)(2,1)S(1)}, s16[136,256]{1,0:T(8,128)(2,1)S(1)}, u32[]{:S(2)}, u32[]{:S(2)}) collective-permute-start(s16[136,256]{1,0:T(8,128)(2,1)S(1)} %get-tuple-element.10), channel_id=1, source_target_pairs={{1,2},{2,1},{3,4},{4,3},{5,6},{6,5},{7,8},{8,7},{9,10},{10,9},{11,... | collective-permute-start | bytes 208904 | tf_op jit(solution)/shard_map/ppermute | solution.py:378

commit v5 on v4

--- a/solution.py
+++ b/solution.py
@@ -197,7 +197,7 @@
     *refs,
     total,
 ):
-    *parts, probe, intensity, row_ref, column_high, column_low, out, near_out, far_out = refs
+    *parts, neighbour_spots, probe, intensity, row_ref, column_high, column_low, out, near_out, far_out = refs
     tile = probe.shape[1]
     reach = tile // 2
     sums_real, sums_imag = [], []
@@ -264,6 +264,9 @@
         rows = slice(part * reach, (part + 1) * reach)
         near_out[rows] = jnp.where(even, value[reach:], value[:reach]).astype(jnp.int16)
         far_out[rows] = jnp.where(even, value[:reach], value[reach:]).astype(jnp.int16)
+    top_row = lax.broadcasted_iota(jnp.int32, head.shape, 0) == 0
+    spots = neighbour_spots[...].astype(jnp.int32)
+    head = jnp.where(top_row, head.astype(jnp.int32), spots).astype(jnp.int16)
     near_out[2 * reach :] = head
     far_out[2 * reach :] = head
 
@@ -401,19 +404,13 @@
     side = odd.reshape(1)
     coded_rows = 2 * tile + HEAD
 
-    spots = jnp.concatenate([positions, angle_index]).astype(jnp.bfloat16)
-    spots = jnp.pad(spots[None], ((0, HEAD - 1), (0, width - 2 * frames)))
+    spots = jnp.concatenate([positions, angle_index]).astype(jnp.int16)
+    spots = jnp.pad(spots[None], ((1, HEAD - 2), (0, width - 2 * frames)))
     rim_rows = 2 * levels * reach
     last = object_field[:, :, reach:].reshape(rim_rows, width)
     first = object_field[:, :, :reach].reshape(rim_rows, width)
-    near = jnp.concatenate([jnp.where(odd == 0, last, first), spots])
-    far = jnp.concatenate([jnp.where(odd == 0, first, last), spots])
-    near = exchanged(near, 0)
-    far = exchanged(far, 1)
-    near_spots = near[rim_rows, : 2 * frames].astype(jnp.int32)
-    far_spots = far[rim_rows, : 2 * frames].astype(jnp.int32)
-    below = jnp.where(odd == 0, far_spots, near_spots)
-    above = jnp.where(odd == 0, near_spots, far_spots)
+    near = exchanged(jnp.where(odd == 0, last, first), 0)
+    far = exchanged(jnp.where(odd == 0, first, last), 1)
     cosines = jnp.cos(depth_phase).reshape(-1)
     sines = jnp.sin(depth_phase).reshape(-1)
 
@@ -443,14 +440,20 @@
             jax.ShapeDtypeStruct((rows, width), jnp.int16)
             for rows in (coded_rows, half_rows, half_rows)
         ],
-        in_specs=[scalars()] * 3 + [resident()] * 6,
+        in_specs=[scalars()] * 3 + [resident()] * 7,
         out_specs=[resident()] * 3,
         compiler_params=params(16),
         interpret=INTERPRET,
         name="far_field",
-    )(slab, side, frame_count, received, probe_field, intensity, table, column_high, column_low)
-
-    bundle = jnp.concatenate([back, exchanged(near, 0), exchanged(far, 1)])
+    )(slab, side, frame_count, received, spots, probe_field, intensity, table, column_high, column_low)
+
+    near = exchanged(near, 0)
+    far = exchanged(far, 1)
+    near_spots = near[tile + 1, : 2 * frames].astype(jnp.int32)
+    far_spots = far[tile + 1, : 2 * frames].astype(jnp.int32)
+    below = jnp.where(odd == 0, far_spots, near_spots)
+    above = jnp.where(odd == 0, near_spots, far_spots)
+    bundle = jnp.concatenate([back, near, far])
     gathered = lax.all_gather(bundle, "depth")
 
     return pl.pallas_call(

time: 86.8 us -> 86.1 us (level)
  the two profiles are of different devices: /device:TPU:257 before, /device:TPU:385 now
where the time goes in v5:
time: 86.1 us; the launch traced here: 85.9 us
  waiting for transfers between devices  29.6 us (34%)
  starting transfers between devices  22.2 us (26%)
  blocking collectives  18 us (21%)
  Pallas kernels  13.2 us (15%)
  other arithmetic  1.47 us (2%)
    all_gather x1, blocking collectives, shards(): gathered = lax.all_gather(bundle, 'depth')  18 us
    ppermute x4, starting transfers between devices, exchanged(): lax.ppermute(value, 'lat', [(i, j) for i, j in pairs if 0 <= j < count])  16.1 us
    ppermute x4, waiting for transfers between devices, exchanged(): lax.ppermute(value, 'lat', [(i, j) for i, j in pairs if 0 <= j < count])  14.9 us
    all_to_all x1, waiting for transfers between devices, shards(): received = lax.all_to_all(partials, 'depth', 0, 0)  14.7 us
    pallas_call x1, Pallas kernels, shards(): pl.pallas_call(correction_kernel, out_shape=jax.ShapeDtypeStruct((2, leve...  6.52 us
    all_to_all x1, starting transfers between devices, shards(): received = lax.all_to_all(partials, 'depth', 0, 0)  6.17 us
    pallas_call x1, Pallas kernels, shards(): pl.pallas_call(exit_kernel, out_shape=jax.ShapeDtypeStruct((frames, coded...  4.44 us
    pallas_call x1, Pallas kernels, shards(): pl.pallas_call(lambda *refs: frame_kernel(*refs, total=total), out_shape=...  2.26 us
  transfers between devices with their start and end apart: 5, of which 5 were waited for; matrix products, arithmetic and copies ran while one was open for 1% of the time, Pallas kernels for 0%

profile of v5, /device:TPU:385, one launch (start us, length us, event | category | flops | bytes accessed | tf_op | source)
XLA Modules:
  0.0 85.9 jit_solution(3768369864237190789)
XLA Ops:
  0.0 0.0 copy-start.6
  0.0 0.0 copy-start.8
  0.0 1.4 %broadcast_select_fusion = (bf16[2,8,64,256]{3,2,1,0:T(8,128)(2,1)S(1)}, bf16[2,8,64,256]{3,2,1,0:T(8,128)(2,1)S(1)}) fusion(pred[]{:T(512)S(6)} %eq.2, bf16[2,8,128,256]{3,2,1,0:T(8,128)(2,1)} %own.1), kind=kLoop, calls=%fused_computation | loop fusion | flops 524288 | bytes 2097153 | tf_op jit(solution)/shard_map/jit(_where)/select_n | solution.py:413
  1.4 3.2 %collective-permute-start = (bf16[1024,256]{1,0:T(8,128)(2,1)S(1)}, bf16[1024,256]{1,0:T(8,128)(2,1)S(1)}, u32[]{:S(2)}, u32[]{:S(2)}) collective-permute-start(bf16[1024,256]{1,0:T(8,128)(2,1)S(1)} %bitcast.15), channel_id=1, source_target_pairs={{0,1},{1,0},{2,3},{3,2},{4,5},{5,4},{6,7},{7,6},{8,9},{9,8},{10,11... | collective-permute-start | bytes 1572872 | tf_op jit(solution)/shard_map/ppermute | solution.py:381
  4.6 5.5 %collective-permute-start.1 = (bf16[1024,256]{1,0:T(8,128)(2,1)S(1)}, bf16[1024,256]{1,0:T(8,128)(2,1)S(1)}, u32[]{:S(2)}, u32[]{:S(2)}) collective-permute-start(bf16[1024,256]{1,0:T(8,128)(2,1)S(1)} %bitcast.14), channel_id=1, source_target_pairs={{1,2},{2,1},{3,4},{4,3},{5,6},{6,5},{7,8},{8,7},{9,10},{10,9},{11,... | collective-permute-start | bytes 1572872 | tf_op jit(solution)/shard_map/ppermute | solution.py:381
  10.1 0.0 copy-done.9
  10.1 0.1 copy.13
  10.2 0.1 reshape.58.sines
  10.3 0.1 copy.12
  10.4 0.1 reshape.57.cosines
  10.5 5.6 %collective-permute-done.near = bf16[1024,256]{1,0:T(8,128)(2,1)S(1)} collective-permute-done((bf16[1024,256]{1,0:T(8,128)(2,1)S(1)}, bf16[1024,256]{1,0:T(8,128)(2,1)S(1)}, u32[]{:S(2)}, u32[]{:S(2)}) %collective-permute-start) | collective-permute-done | bytes 524320 | tf_op jit(solution)/shard_map/ppermute | solution.py:381
  16.1 6.2 %collective-permute-done.1.far = bf16[1024,256]{1,0:T(8,128)(2,1)S(1)} collective-permute-done((bf16[1024,256]{1,0:T(8,128)(2,1)S(1)}, bf16[1024,256]{1,0:T(8,128)(2,1)S(1)}, u32[]{:S(2)}, u32[]{:S(2)}) %collective-permute-start.1) | collective-permute-done | bytes 524320 | tf_op jit(solution)/shard_map/ppermute | solution.py:381
  22.3 0.0 copy-done
  22.3 0.0 copy-done.7
  22.3 0.0 copy-start.1
  22.3 0.0 copy-start.2
  22.3 0.0 copy-start.3
  22.4 0.0 copy-start.4
  22.4 0.0 copy-start.5
  22.4 4.4 %exit_waves.1 = s16[8,264,256]{2,1,0:T(8,128)(2,1)} custom-call(s32[1]{0:T(128)} %bitcast.slab.refs_0_, s32[1]{0:T(128)} %bitcast.1.side.refs_1_, s32[8]{0:T(128)S(1)} %copy-done.6, s32[8]{0:T(128)S(1)} %copy-done.7, s32[32]{0:T(128)S(1)} %copy-done.8, f32[256]{0:T(256)S(1)} %reshape.57.cosines, f32[256]{0:T(256)S(1)} %reshape.58.sines, ...), custom_call_target="tpu_custom_call" | custom-call | tf_op jit(solution)/shard_map/exit_waves/pallas_call | solution.py:417
  26.8 6.2 %all-to-all-start = ((s16[8,264,256]{2,1,0:T(8,128)(2,1)}), s16[8,264,256]{2,1,0:T(8,128)(2,1)S(1)}, u32[]{:S(2)}, u32[]{:S(2)}) async-start(s16[8,264,256]{2,1,0:T(8,128)(2,1)} %exit_waves.1), calls=%async_computation | async-start | bytes 2162688 | tf_op jit(solution)/shard_map/all_to_all | solution.py:432
  33.7 0.1 pad_add_fusion.1
  33.8 14.7 %all-to-all-done.refs_3_ = s16[8,264,256]{2,1,0:T(8,128)(2,1)S(1)} async-done(((s16[8,264,256]{2,1,0:T(8,128)(2,1)}), s16[8,264,256]{2,1,0:T(8,128)(2,1)S(1)}, u32[]{:S(2)}, u32[]{:S(2)}) %all-to-all-start) | async-done | bytes 1081376 | tf_op jit(solution)/shard_map/all_to_all | solution.py:432
  48.5 0.0 copy-done.4
  48.5 0.0 copy-done.5
  48.5 2.3 %far_field.1 = (s16[264,256]{1,0:T(8,128)(2,1)S(1)}, s16[136,256]{1,0:T(8,128)(2,1)S(1)}, s16[136,256]{1,0:T(8,128)(2,1)S(1)}) custom-call(s32[1]{0:T(128)} %bitcast.slab.refs_0_, s32[1]{0:T(128)} %bitcast.1.side.refs_1_, s32[1]{0:T(128)S(6)} %copy.14.refs_2_, s16[8,264,256]{2,1,0:T(8,128)(2,1)S(1)} %all-to-all-done.refs_3_, s16[8,256]{1,0:T(8,128)(2,1)S(1)} %pad.4.refs_4_, ...), custom_call_target="tpu_custom_call" | custom-call | tf_op jit(solution)/shard_map/far_field/pallas_call | solution.py:437
  50.8 5.5 %collective-permute-start.2 = (s16[136,256]{1,0:T(8,128)(2,1)S(1)}, s16[136,256]{1,0:T(8,128)(2,1)S(1)}, u32[]{:S(2)}, u32[]{:S(2)}) collective-permute-start(s16[136,256]{1,0:T(8,128)(2,1)S(1)} %get-tuple-element.8), channel_id=1, source_target_pairs={{1,2},{2,1},{3,4},{4,3},{5,6},{6,5},{7,8},{8,7},{9,10},{10,9},{11,... | collective-permute-start | bytes 208904 | tf_op jit(solution)/shard_map/ppermute | solution.py:381
  56.2 1.9 %collective-permute-start.3 = (s16[136,256]{1,0:T(8,128)(2,1)S(1)}, s16[136,256]{1,0:T(8,128)(2,1)S(1)}, u32[]{:S(2)}, u32[]{:S(2)}) collective-permute-start(s16[136,256]{1,0:T(8,128)(2,1)S(1)} %get-tuple-element.9), channel_id=1, source_target_pairs={{0,1},{1,0},{2,3},{3,2},{4,5},{5,4},{6,7},{7,6},{8,9},{9,8},{10,11... | collective-permute-start | bytes 208904 | tf_op jit(solution)/shard_map/ppermute | solution.py:381
  58.2 1.0 %collective-permute-done.2 = s16[136,256]{1,0:T(8,128)(2,1)S(1)} collective-permute-done((s16[136,256]{1,0:T(8,128)(2,1)S(1)}, s16[136,256]{1,0:T(8,128)(2,1)S(1)}, u32[]{:S(2)}, u32[]{:S(2)}) %collective-permute-start.2) | collective-permute-done | bytes 69664 | tf_op jit(solution)/shard_map/ppermute | solution.py:381
  59.1 2.1 %collective-permute-done.3 = s16[136,256]{1,0:T(8,128)(2,1)S(1)} collective-permute-done((s16[136,256]{1,0:T(8,128)(2,1)S(1)}, s16[136,256]{1,0:T(8,128)(2,1)S(1)}, u32[]{:S(2)}, u32[]{:S(2)}) %collective-permute-start.3) | collective-permute-done | bytes 69664 | tf_op jit(solution)/shard_map/ppermute | solution.py:381
  61.3 18.0 %all-gather.2 = s16[4288,256]{1,0:T(8,128)(2,1)S(1)} all-gather(s16[536,256]{1,0:T(8,128)(2,1)S(1)} %pad_add_fusion), channel_id=2, replica_groups=mesh['depth'=8,'lat'=64] {'depth'}, dimensions={0}, use_global_device_ids=true | all-gather | bytes 2469888 | tf_op jit(solution)/shard_map/all_gather | solution.py:457
  79.3 6.5 %corrections.1 = f32[2,8,128,256]{3,2,1,0:T(8,128)} custom-call(s32[1]{0:T(128)} %bitcast.slab.refs_0_, s32[1]{0:T(128)} %bitcast.1.side.refs_1_, s32[8]{0:T(128)S(1)} %copy-done.6, s32[8]{0:T(128)S(1)} %copy-done.7, s32[16]{0:T(128)S(1)} %get-tuple-element.14.below, s32[16]{0:T(128)S(1)} %get-tuple-element.13.above, s32[32]{0:T(128)S(1)} %copy-done.8, ...), custom_call_target="tpu_custom_call" | custom-call | tf_op jit(solution)/shard_map/corrections/pallas_call | solution.py:459
  (13 shorter events, 0.1 us)
Async XLA Ops:
  0.0 22.3 %copy-start = (bf16[2,8,128,256]{3,2,1,0:T(8,128)(2,1)S(1)}, bf16[2,8,128,256]{3,2,1,0:T(8,128)(2,1)}, u32[]{:S(2)}) copy-start(bf16[2,8,128,256]{3,2,1,0:T(8,128)(2,1)} %own.1) | copy-start | bytes 3145732
  0.0 10.1 %copy-start.9 = (f32[32,8]{0,1:T(8,128)S(1)}, f32[32,8]{0,1:T(8,128)}, u32[]{:S(2)}) copy-start(f32[32,8]{0,1:T(8,128)} %param.14) | copy-start | bytes 3076
  0.0 22.3 %copy-start.7 = (s32[8]{0:T(128)S(1)}, s32[8]{0:T(128)}, u32[]{:S(2)}) copy-start(s32[8]{0:T(128)} %angles.3) | copy-start | bytes 100
  0.0 22.3 %copy-start.6 = (s32[8]{0:T(128)S(1)}, s32[8]{0:T(128)}, u32[]{:S(2)}) copy-start(s32[8]{0:T(128)} %positions.3) | copy-start | bytes 100
  0.0 22.3 %copy-start.8 = (s32[32]{0:T(128)S(1)}, s32[32]{0:T(128)}, u32[]{:S(2)}) copy-start(s32[32]{0:T(128)} %shears.3) | copy-start | bytes 388
  1.4 14.7 %collective-permute-start = (bf16[1024,256]{1,0:T(8,128)(2,1)S(1)}, bf16[1024,256]{1,0:T(8,128)(2,1)S(1)}, u32[]{:S(2)}, u32[]{:S(2)}) collective-permute-start(bf16[1024,256]{1,0:T(8,128)(2,1)S(1)} %bitcast.15), channel_id=1, source_target_pairs={{0,1},{1,0},{2,3},{3,2},{4,5},{5,4},{6,7},{7,6},{8,9},{9,8},{10,11... | collective-permute-start | bytes 1572872 | tf_op jit(solution)/shard_map/ppermute | solution.py:381
  4.6 17.7 %collective-permute-start.1 = (bf16[1024,256]{1,0:T(8,128)(2,1)S(1)}, bf16[1024,256]{1,0:T(8,128)(2,1)S(1)}, u32[]{:S(2)}, u32[]{:S(2)}) collective-permute-start(bf16[1024,256]{1,0:T(8,128)(2,1)S(1)} %bitcast.14), channel_id=1, source_target_pairs={{1,2},{2,1},{3,4},{4,3},{5,6},{6,5},{7,8},{8,7},{9,10},{10,9},{11,... | collective-permute-start | bytes 1572872 | tf_op jit(solution)/shard_map/ppermute | solution.py:381
  22.3 26.1 %copy-start.1 = (bf16[8,128,256]{2,1,0:T(8,128)(2,1)S(1)}, bf16[8,128,256]{2,1,0:T(8,128)(2,1)}, u32[]{:S(2)}) copy-start(bf16[8,128,256]{2,1,0:T(8,128)(2,1)} %refs_6_.1) | copy-start | bytes 1572868
  22.3 26.1 %copy-start.2 = (bf16[256,512]{1,0:T(8,128)(2,1)S(1)}, bf16[256,512]{1,0:T(8,128)(2,1)}, u32[]{:S(2)}) copy-start(bf16[256,512]{1,0:T(8,128)(2,1)} %constant.23.clone.refs_9_) | copy-start | bytes 786436
  22.3 26.1 %copy-start.3 = (bf16[256,512]{1,0:T(8,128)(2,1)S(1)}, bf16[256,512]{1,0:T(8,128)(2,1)}, u32[]{:S(2)}) copy-start(bf16[256,512]{1,0:T(8,128)(2,1)} %constant.22.clone.refs_8_) | copy-start | bytes 786436
  22.4 26.1 %copy-start.4 = (bf16[256,384]{1,0:T(8,128)(2,1)S(1)}, bf16[256,384]{1,0:T(8,128)(2,1)}, u32[]{:S(2)}) copy-start(bf16[256,384]{1,0:T(8,128)(2,1)} %constant.21.clone.refs_7_) | copy-start | bytes 589828
  22.4 26.1 %copy-start.5 = (bf16[2,128,256]{2,1,0:T(8,128)(2,1)S(1)}, bf16[2,128,256]{2,1,0:T(8,128)(2,1)}, u32[]{:S(2)}) copy-start(bf16[2,128,256]{2,1,0:T(8,128)(2,1)} %refs_5_.1) | copy-start | bytes 393220
  26.8 21.6 %all-to-all-start = ((s16[8,264,256]{2,1,0:T(8,128)(2,1)}), s16[8,264,256]{2,1,0:T(8,128)(2,1)S(1)}, u32[]{:S(2)}, u32[]{:S(2)}) async-start(s16[8,264,256]{2,1,0:T(8,128)(2,1)} %exit_waves.1), calls=%async_computation | async-start | bytes 2162688 | tf_op jit(solution)/shard_map/all_to_all | solution.py:432
  50.8 8.4 %collective-permute-start.2 = (s16[136,256]{1,0:T(8,128)(2,1)S(1)}, s16[136,256]{1,0:T(8,128)(2,1)S(1)}, u32[]{:S(2)}, u32[]{:S(2)}) collective-permute-start(s16[136,256]{1,0:T(8,128)(2,1)S(1)} %get-tuple-element.8), channel_id=1, source_target_pairs={{1,2},{2,1},{3,4},{4,3},{5,6},{6,5},{7,8},{8,7},{9,10},{10,9},{11,... | collective-permute-start | bytes 208904 | tf_op jit(solution)/shard_map/ppermute | solution.py:381
  56.2 5.1 %collective-permute-start.3 = (s16[136,256]{1,0:T(8,128)(2,1)S(1)}, s16[136,256]{1,0:T(8,128)(2,1)S(1)}, u32[]{:S(2)}, u32[]{:S(2)}) collective-permute-start(s16[136,256]{1,0:T(8,128)(2,1)S(1)} %get-tuple-element.9), channel_id=1, source_target_pairs={{0,1},{1,0},{2,3},{3,2},{4,5},{5,4},{6,7},{7,6},{8,9},{9,8},{10,11... | collective-permute-start | bytes 208904 | tf_op jit(solution)/shard_map/ppermute | solution.py:381
